TPU v7x, 128 devices: a whole 4x4x4 slice. The times are simulated.
128 devices in a mesh: grp: 4 (over y), seq: 32 (over z, x, core).
Axes of the slice: x: 4, y: 4, z: 4, core: 2. Of those that a mesh axis runs over, the one named last changes fastest.
Arguments:
- tiles: bfloat16 [8, 16384, 768], P('grp', 'seq'), may hold values from -8 to 8
- counts: int32 [8], P('grp'), may hold values from 4096 to 16384, as said below
- ln1_gain: float32 [768], replicated, may hold values from 0.1 to 1.9
- qkv_weight: bfloat16 [768, 2304], replicated, may hold values from -0.18042196 to 0.18042196
- out_weight: bfloat16 [768, 768], replicated, may hold values from -0.21875 to 0.21875
- ln2_gain: float32 [768], replicated, may hold values from 0.1 to 1.9
- ff_in: bfloat16 [768, 3072], replicated, may hold values from -0.21875 to 0.21875
- ff_out: bfloat16 [3072, 768], replicated, may hold values from -0.109375 to 0.109375
- pool_weight: bfloat16 [768, 768], P('grp'), may hold values from -0.18042196 to 0.18042196
- class_weight: float32 [384, 8], replicated, may hold values from -3 to 6
Outputs:
- encoded: bfloat16 [8, 16384, 768], P('grp', 'seq')
- pooled: float32 [8, 8, 768], P('grp')
Inputs may be any that keep to these rules, and one draw needn't show every extreme that they name: The valid tiles of a slide are its first counts tiles in scan order; some slide has all 16384 tiles valid.
All inputs are finite; a program needn't handle non-finite values.
Results may differ from a plain program's by a relative error of at most 0.015.
Values may be sent and summed in bfloat16 or wider, within the bound.
No kernel may reach another device: no remote copies, remote signals or barrier semaphores. Data moves between devices by JAX's collectives and lax.ppermute only.
A program may use at most 128 MiB of HBM per device.

v0:
```python
import jax
import jax.numpy as jnp
from jax import lax
from jax.sharding import Mesh
from jax.sharding import PartitionSpec as P

HEADS = 16
BLOCK = 256
SEQ = ("seq_0", "seq_1", "seq_2")


def sent_to_all(x, axis):
    size = lax.axis_size(axis)
    return lax.all_to_all(jnp.broadcast_to(x[None], (size, *x.shape)), axis, 0, 0, tiled=True)


def laid_out(parts, dim):
    parts = jnp.moveaxis(parts, 0, dim)
    dims = parts.shape
    return parts.reshape(*dims[:dim], dims[dim] * dims[dim + 1], *dims[dim + 2 :])


def collect(x, axis, dim):
    parts = sent_to_all(x, axis)
    return laid_out(parts, dim)


def gathered_once(x, axis):
    leaves = jax.tree.leaves(x)
    sequence = sorted(range(len(leaves)), key=lambda k: -leaves[k].size)
    width = (1, *leaves[sequence[0]].shape)[-1]
    lines = [
        jnp.pad(leaves[k].reshape(-1), (0, -leaves[k].size % width)).reshape(-1, width)
        for k in sequence
    ]
    both, at, found = (lax.all_gather(jnp.concatenate(lines), axis), 0, {})
    for k, line in zip(sequence, lines):
        section = both[:, at : at + len(line)].reshape(len(both), -1)
        found[k] = section[:, : leaves[k].size].reshape(-1, *leaves[k].shape)
        at += len(line)
    numbers = iter(range(len(leaves)))
    return jax.tree.map(lambda _: found[next(numbers)], x)


def joined_all(x, axes, combine):
    for axis in axes:
        pieces = gathered_once(x, axis)
        x = jax.tree.map(lambda part: part[0], pieces)
        for k in range(1, lax.axis_size(axis)):
            x = combine(x, jax.tree.map(lambda part: part[k], pieces))
    return x


def normalize(values, gain):
    xf = values.astype(jnp.float32)
    centre = jnp.mean(xf, axis=-1, keepdims=True)
    spread = jnp.mean((xf - centre) ** 2, axis=-1, keepdims=True)
    return (xf - centre) * lax.rsqrt(spread + 1e-05) * gain


def attend(query, key_rows, value_rows, keep):
    scale = 1.0 / query.shape[-1] ** 0.5
    scores = jnp.einsum("qhd,khd->hqk", query, key_rows, preferred_element_type=jnp.float32) * scale
    scores = jnp.where(keep[None, None, :], scores, -1e30)
    peak = jnp.max(scores, axis=-1)
    probs = jnp.exp(scores - peak[..., None])
    total = jnp.sum(probs, axis=-1)
    result = jnp.einsum(
        "hqk,khd->qhd", probs.astype(jnp.bfloat16), value_rows, preferred_element_type=jnp.float32
    )
    return (result / total.T[..., None], (peak + jnp.log(total)).T)


def near_branch(proj, valid, width, heads):
    slides, rows = (proj.shape[0], proj.shape[1])
    head_dim = width // heads
    nblocks = slides * rows // BLOCK
    query = proj[:, :, :width].reshape(nblocks, BLOCK, heads, head_dim)
    key_rows = proj[:, :, width : 2 * width].reshape(nblocks, BLOCK, heads, head_dim)
    value_rows = proj[:, :, 2 * width :].reshape(nblocks, BLOCK, heads, head_dim)

    def step(item):
        return attend(item[0], item[1], item[2], item[3])

    result, lse = lax.map(step, (query, key_rows, value_rows, valid.reshape(nblocks, BLOCK)))
    return (result.reshape(slides, rows, heads, head_dim), lse.reshape(slides, rows, heads))


def far_branch(proj, keep, width, heads):
    slides, rows = (proj.shape[0], proj.shape[1])
    head_dim = width // heads
    qblocks = rows // BLOCK

    def per_slide(item):
        rows_proj, rows_keep = item
        key_rows = rows_proj[:, width : 2 * width].reshape(rows, heads, head_dim)
        value_rows = rows_proj[:, 2 * width :].reshape(rows, heads, head_dim)

        def per_block(query):
            return attend(query, key_rows, value_rows, rows_keep)

        query = rows_proj[:, :width].reshape(qblocks, BLOCK, heads, head_dim)
        result, lse = lax.map(per_block, query)
        return (result.reshape(rows, width).astype(jnp.bfloat16), lse.reshape(rows, heads))

    return lax.map(per_slide, (proj, keep))


def fold_pair(first, second):
    top = jnp.maximum(first[0], second[0])
    wone = jnp.exp(first[0] - top)
    wtwo = jnp.exp(second[0] - top)
    return (
        top,
        wone * first[1] + wtwo * second[1],
        wone[..., None] * first[2] + wtwo[..., None] * second[2],
    )


def local(
    tiles,
    counts,
    ln1_gain,
    qkv_weight,
    out_weight,
    ln2_gain,
    ff_in,
    ff_out,
    pool_weight,
    class_weight,
):
    slides, rows, width = tiles.shape
    heads = HEADS
    head_dim = width // heads
    ratio = lax.axis_size(SEQ)
    here = lax.axis_index(SEQ)
    positions = jnp.arange(rows, dtype=jnp.int32)
    valid = (here * rows + positions)[None, :] < counts[:, None]
    class_keep = (positions * ratio + here)[None, :] < counts[:, None]
    normed = normalize(tiles, ln1_gain).astype(jnp.bfloat16)
    proj = (
        jnp.dot(normed.reshape(-1, width), qkv_weight, preferred_element_type=jnp.float32)
        .astype(jnp.bfloat16)
        .reshape(slides, rows, 3 * width)
    )
    moved = lax.all_to_all(
        normed.reshape(slides, rows // ratio, ratio, width),
        SEQ,
        split_axis=2,
        concat_axis=1,
        tiled=True,
    )
    spread = (
        jnp.dot(moved.reshape(-1, width), qkv_weight, preferred_element_type=jnp.float32)
        .astype(jnp.bfloat16)
        .reshape(slides, rows, 3 * width)
    )
    far_out, far_lse = far_branch(spread, class_keep, width, heads)
    back_out = lax.all_to_all(
        far_out.reshape(slides, rows, 1, width), SEQ, split_axis=1, concat_axis=2, tiled=True
    )
    back_lse = lax.all_to_all(
        far_lse.reshape(slides, rows, 1, heads), SEQ, split_axis=1, concat_axis=2, tiled=True
    )
    back_out = back_out.reshape(slides, rows, heads, head_dim).astype(jnp.float32)
    back_lse = back_lse.reshape(slides, rows, heads)
    near_out, near_lse = near_branch(proj, valid, width, heads)
    top = jnp.maximum(near_lse, back_lse)
    near_w = jnp.exp(near_lse - top)
    far_w = jnp.exp(back_lse - top)
    mixed = (near_w[..., None] * near_out + far_w[..., None] * back_out) / (near_w + far_w)[
        ..., None
    ]
    mixed = mixed.reshape(-1, width).astype(jnp.bfloat16)
    resid = tiles.reshape(-1, width).astype(jnp.float32) + jnp.dot(
        mixed, out_weight, preferred_element_type=jnp.float32
    )
    normed2 = normalize(resid, ln2_gain).astype(jnp.bfloat16)
    act = jax.nn.gelu(
        jnp.dot(normed2, ff_in, preferred_element_type=jnp.float32), approximate=False
    ).astype(jnp.bfloat16)
    encoded = (resid + jnp.dot(act, ff_out, preferred_element_type=jnp.float32)).astype(
        jnp.bfloat16
    )
    flat_valid = valid.reshape(-1)
    encoded = jnp.where(flat_valid[:, None], encoded, jnp.zeros_like(encoded))
    zed = jnp.dot(encoded, collect(pool_weight, "grp", 0), preferred_element_type=jnp.float32)
    hidden = pool_weight.shape[1] // 2
    gate = jnp.tanh(zed[:, :hidden]) * jax.nn.sigmoid(zed[:, hidden:])
    logits = jnp.dot(gate, class_weight, precision=lax.Precision.HIGHEST).reshape(slides, rows, -1)
    logits = jnp.where(valid[..., None], logits, -1e30)
    local_peak = jnp.max(logits, axis=1)
    mask_float = valid[..., None].astype(jnp.float32)
    enc_float = encoded.reshape(slides, rows, width).astype(jnp.float32)
    expo = jnp.exp(logits - local_peak[:, None, :]) * mask_float
    numer = jnp.einsum("stc,std->scd", expo, enc_float, precision=lax.Precision.HIGHEST)
    peak, total, numer = joined_all((local_peak, jnp.sum(expo, axis=1), numer), SEQ, fold_pair)
    pooled = numer / total[..., None]
    return (encoded.reshape(slides, rows, width), pooled)


def solution(mesh):
    torus = Mesh(
        mesh.devices.reshape(mesh.shape["grp"], 4, 4, 2), ("grp", "seq_0", "seq_1", "seq_2")
    )
    return jax.shard_map(
        local,
        mesh=torus,
        in_specs=(P("grp", SEQ, None), P("grp"), P(), P(), P(), P(), P(), P(), P("grp", None), P()),
        out_specs=(P("grp", SEQ, None), P("grp", None, None)),
        check_vma=False,
    )
```

profile of v0, /device:TPU:1, one launch (start us, length us, event | category | flops | bytes accessed | tf_op | source)
XLA Modules:
  0.0 403.3 jit_solution(11059577748910741996)
XLA Ops:
  9.1 10.2 %all-to-all-start = ((bf16[2,16,32,768]{3,1,0,2:T(8,128)(2,1)}), bf16[2,16,32,768]{3,1,0,2:T(8,128)(2,1)}, u32[]{:S(2)}, u32[]{:S(2)}) async-start(bf16[2,16,32,768]{3,1,0,2:T(8,128)(2,1)} %copy.88), calls=%async_computation | async-start | bytes 3145728 | tf_op jit(solution)/shard_map/all_to_all | solution.py:146
  21.3 5.9 %convolution_convert_fusion.1 = bf16[1024,2304]{1,0:T(8,128)(2,1)S(1)} fusion(bf16[1024,768]{1,0:T(8,128)(2,1)} %bitcast.440, bf16[768,2304]{1,0:T(8,128)(2,1)S(1)} %copy-done), kind=kOutput, calls=%fused_computation.68 | convolution fusion | flops 3626237952 | bytes 9830400 | tf_op jit(solution)/shard_map/dot_general | solution.py:142
  29.3 12.0 %all-to-all-done = bf16[2,16,32,768]{3,1,0,2:T(8,128)(2,1)} async-done(((bf16[2,16,32,768]{3,1,0,2:T(8,128)(2,1)}), bf16[2,16,32,768]{3,1,0,2:T(8,128)(2,1)}, u32[]{:S(2)}, u32[]{:S(2)}) %all-to-all-start) | async-done | bytes 1572896 | tf_op jit(solution)/shard_map/all_to_all | solution.py:146
  42.8 5.5 %convolution_convert_fusion = bf16[1024,2304]{1,0:T(8,128)(2,1)} fusion(bf16[1024,768]{1,0:T(8,128)(2,1)S(1)} %bitcast.446, bf16[768,2304]{1,0:T(8,128)(2,1)S(1)} %copy-done), kind=kOutput, calls=%fused_computation.67 | convolution fusion | flops 3626237952 | bytes 9830400 | tf_op jit(solution)/shard_map/dot_general | solution.py:154
  48.3 66.9 %while.38 = (s32[]{:T(128)}, bf16[2,512,768]{1,2,0:T(8,128)(2,1)}, f32[2,512,16]{1,2,0:T(8,128)}, bf16[2,512,2304]{2,1,0:T(8,128)(2,1)}, pred[2,512]{1,0:T(4,128...) while((s32[]{:T(128)}, bf16[2,512,768]{1,2,0:T(8,128)(2,1)}, f32[2,512,16]{1,2,0:T(8,128)}, ...), condition=%wide.region_11.12_spmd, body=%wide.region_6.11_spmd.sunk | while | flops 425914368 | bytes 87494024 | solution.py:106
  58.1 20.6 %while.39 = (s32[]{:T(128)}, bf16[2,256,16,48]{1,3,2,0:T(8,128)(2,1)S(1)}, f32[2,256,16]{1,0,2:T(2,128)S(1)}, pred[512]{0:T(512)(128)(4,1)S(1)}, bf16[2,256,16,4...) while((s32[]{:T(128)}, ...), condition=%wide.region_10.10_spmd, body=%wide.region_7.9_spmd.sunk | while | flops 425914368 | bytes 64816800 | solution.py:103
  63.1 5.3 %fusion.224 = bf16[2,256,16,48]{1,3,2,0:T(8,128)(2,1)S(1)} fusion(bf16[2,256,16,48]{1,3,2,0:T(8,128)(2,1)S(1)} %get-tuple-element.438, s32[]{:T(128)} %get-tuple-element.437, bf16[512,16,48]{0,2,1:T(8,128)(2,1)S(1)} %copy-done.5, f32[16,256,512]{2,1,0:T(8,128)} %copy-done.2, f32[16,256]{1,0:T(8,128)S(1)} %get-tuple-element.427, ...), kind=kOutput, calls=%fused_computation.10.clone.1 | convolution fusion | flops 209911808 | bytes 9994756 | tf_op jit(solution)/shard_map/while/body/eval_jaxpr/while/body/eval_jaxpr/hqk,khd->qhd/dot_general | solution.py:68
  73.4 5.3 %fusion.224 = bf16[2,256,16,48]{1,3,2,0:T(8,128)(2,1)S(1)} fusion(bf16[2,256,16,48]{1,3,2,0:T(8,128)(2,1)S(1)} %get-tuple-element.438, s32[]{:T(128)} %get-tuple-element.437, bf16[512,16,48]{0,2,1:T(8,128)(2,1)S(1)} %copy-done.5, f32[16,256,512]{2,1,0:T(8,128)} %copy-done.2, f32[16,256]{1,0:T(8,128)S(1)} %get-tuple-element.427, ...), kind=kOutput, calls=%fused_computation.10.clone.1 | convolution fusion | flops 209911808 | bytes 9994756 | tf_op jit(solution)/shard_map/while/body/eval_jaxpr/while/body/eval_jaxpr/hqk,khd->qhd/dot_general | solution.py:68
  91.5 20.6 %while.39 = (s32[]{:T(128)}, bf16[2,256,16,48]{1,3,2,0:T(8,128)(2,1)S(1)}, f32[2,256,16]{1,0,2:T(2,128)S(1)}, pred[512]{0:T(512)(128)(4,1)S(1)}, bf16[2,256,16,4...) while((s32[]{:T(128)}, ...), condition=%wide.region_10.10_spmd, body=%wide.region_7.9_spmd.sunk | while | flops 425914368 | bytes 64816800 | solution.py:103
  96.4 5.3 %fusion.224 = bf16[2,256,16,48]{1,3,2,0:T(8,128)(2,1)S(1)} fusion(bf16[2,256,16,48]{1,3,2,0:T(8,128)(2,1)S(1)} %get-tuple-element.438, s32[]{:T(128)} %get-tuple-element.437, bf16[512,16,48]{0,2,1:T(8,128)(2,1)S(1)} %copy-done.5, f32[16,256,512]{2,1,0:T(8,128)} %copy-done.2, f32[16,256]{1,0:T(8,128)S(1)} %get-tuple-element.427, ...), kind=kOutput, calls=%fused_computation.10.clone.1 | convolution fusion | flops 209911808 | bytes 9994756 | tf_op jit(solution)/shard_map/while/body/eval_jaxpr/while/body/eval_jaxpr/hqk,khd->qhd/dot_general | solution.py:68
  106.7 5.3 %fusion.224 = bf16[2,256,16,48]{1,3,2,0:T(8,128)(2,1)S(1)} fusion(bf16[2,256,16,48]{1,3,2,0:T(8,128)(2,1)S(1)} %get-tuple-element.438, s32[]{:T(128)} %get-tuple-element.437, bf16[512,16,48]{0,2,1:T(8,128)(2,1)S(1)} %copy-done.5, f32[16,256,512]{2,1,0:T(8,128)} %copy-done.2, f32[16,256]{1,0:T(8,128)S(1)} %get-tuple-element.427, ...), kind=kOutput, calls=%fused_computation.10.clone.1 | convolution fusion | flops 209911808 | bytes 9994756 | tf_op jit(solution)/shard_map/while/body/eval_jaxpr/while/body/eval_jaxpr/hqk,khd->qhd/dot_general | solution.py:68
  117.7 5.5 %all-to-all-start.1 = ((f32[32,1,512]{2,1,0:T(1,128)}), f32[32,1,512]{2,1,0:T(1,128)S(1)}, u32[]{:S(2)}, u32[]{:S(2)}) async-start(f32[32,1,512]{2,1,0:T(1,128)} %reshape.712), calls=%async_computation.1 | async-start | bytes 131072 | tf_op jit(solution)/shard_map/all_to_all | solution.py:162
  145.6 5.0 %copy.99 = bf16[2,512,768]{2,0,1:T(2,128)(2,1)} copy(bf16[2,512,768]{1,2,0:T(8,128)(2,1)} %get-tuple-element.109) | data formatting | bytes 3145728 | tf_op jit(solution)/shard_map/while | solution.py:106
  150.5 7.5 %all-to-all-start.2 = ((bf16[2,512,1,768]{3,0,2,1:T(2,128)(2,1)}), bf16[2,512,1,768]{3,0,2,1:T(2,128)(2,1)}, u32[]{:S(2)}, u32[]{:S(2)}) async-start(bf16[2,512,1,768]{3,0,2,1:T(2,128)(2,1)} %bitcast.29), calls=%async_computation.2 | async-start | bytes 3145728 | tf_op jit(solution)/shard_map/all_to_all | solution.py:159
  158.1 117.7 %while.36 = (s32[]{:T(128)}, f32[4,256,16,48]{1,0,3,2:T(4,128)}, f32[4,256,16]{1,0,2:T(4,128)S(1)}, bf16[4,256,16,48]{1,3,2,0:T(8,128)(2,1)}, pred[4,256]{1,0:T(...) while((s32[]{:T(128)}, f32[4,256,16,48]{1,0,3,2:T(4,128)}, ...), condition=%wide.region_5.6_spmd, body=%wide.region_2.5_spmd.sunk | while | flops 213053440 | bytes 17894504 | solution.py:85
  164.1 23.2 %dynamic_update_slice.33 = f32[4,256,16,48]{1,0,3,2:T(4,128)} dynamic-update-slice(f32[4,256,16,48]{1,0,3,2:T(4,128)} %get-tuple-element.492, f32[1,256,16,48]{1,0,3,2:T(1,128)S(1)} %copy.160, s32[]{:T(128)} %get-tuple-element.491, s32[]{:T(128)} %constant.41.clone.1..sunk, s32[]{:T(128)} %constant.41.clone.1..sunk, s32[]{:T(128)} %constant.41.clone.1..sunk) | dynamic-update-slice | bytes 1572868 | tf_op jit(solution)/shard_map/while/body/jit(dynamic_update_index_in_dim)/dynamic_update_slice | solution.py:85
  193.5 23.2 %dynamic_update_slice.33 = f32[4,256,16,48]{1,0,3,2:T(4,128)} dynamic-update-slice(f32[4,256,16,48]{1,0,3,2:T(4,128)} %get-tuple-element.492, f32[1,256,16,48]{1,0,3,2:T(1,128)S(1)} %copy.160, s32[]{:T(128)} %get-tuple-element.491, s32[]{:T(128)} %constant.41.clone.1..sunk, s32[]{:T(128)} %constant.41.clone.1..sunk, s32[]{:T(128)} %constant.41.clone.1..sunk) | dynamic-update-slice | bytes 1572868 | tf_op jit(solution)/shard_map/while/body/jit(dynamic_update_index_in_dim)/dynamic_update_slice | solution.py:85
  222.9 23.2 %dynamic_update_slice.33 = f32[4,256,16,48]{1,0,3,2:T(4,128)} dynamic-update-slice(f32[4,256,16,48]{1,0,3,2:T(4,128)} %get-tuple-element.492, f32[1,256,16,48]{1,0,3,2:T(1,128)S(1)} %copy.160, s32[]{:T(128)} %get-tuple-element.491, s32[]{:T(128)} %constant.41.clone.1..sunk, s32[]{:T(128)} %constant.41.clone.1..sunk, s32[]{:T(128)} %constant.41.clone.1..sunk) | dynamic-update-slice | bytes 1572868 | tf_op jit(solution)/shard_map/while/body/jit(dynamic_update_index_in_dim)/dynamic_update_slice | solution.py:85
  252.3 23.2 %dynamic_update_slice.33 = f32[4,256,16,48]{1,0,3,2:T(4,128)} dynamic-update-slice(f32[4,256,16,48]{1,0,3,2:T(4,128)} %get-tuple-element.492, f32[1,256,16,48]{1,0,3,2:T(1,128)S(1)} %copy.160, s32[]{:T(128)} %get-tuple-element.491, s32[]{:T(128)} %constant.41.clone.1..sunk, s32[]{:T(128)} %constant.41.clone.1..sunk, s32[]{:T(128)} %constant.41.clone.1..sunk) | dynamic-update-slice | bytes 1572868 | tf_op jit(solution)/shard_map/while/body/jit(dynamic_update_index_in_dim)/dynamic_update_slice | solution.py:85
  307.7 8.5 %fusion.183 = (f32[1024]{0:T(1024)S(1)}, f32[1024,768]{1,0:T(8,128)S(1)}) fusion(bf16[768,768]{1,0:T(8,128)(2,1)S(1)} %copy-done.11, f32[1024,768]{0,1:T(8,128)} %bitcast.436, f32[1024,768]{0,1:T(8,128)} %bitcast.438, f32[1024,768]{0,1:T(8,128)} %copy.102, f32[1024,768]{0,1:T(8,128)} %bitcast.437, f32[1024,768]{0,1:T(8,128)} %bitcast.435, ...), kind=kOutput, calls=%fused_computation.254 | convolution fusion | flops 1214249984 | bytes 21630976 | tf_op jit(solution)/shard_map/dot_general | solution.py:175
  318.4 39.2 %broadcast_select_fusion = bf16[1024,768]{1,0:T(8,128)(2,1)S(1)} fusion(pred[1024]{0:T(1024)(128)(4,1)S(1)} %lt.63, f32[1024,768]{1,0:T(8,128)} %copy-done.6, bf16[3072,768]{1,0:T(8,128)(2,1)} %param.23, bf16[768,3072]{1,0:T(8,128)(2,1)} %param.22, f32[768]{0:T(1024)S(1)} %copy-done.23, f32[1024]{0:T(1024)S(1)} %add_rsqrt_fusion, ...), kind=kOutput, calls=%fused_computation.88 | convolution fusion | flops 9873653760 | bytes 14168064 | tf_op jit(solution)/shard_map/dot_general | solution.py:182
  370.0 10.4 %all-gather.3 = f32[4,18,768]{2,1,0:T(8,128)S(1)} all-gather(f32[1,18,768]{2,1,0:T(8,128)S(1)} %maximum_bitcast_fusion), channel_id=2, replica_groups=mesh['grp'=4,'seq_0'=4,'seq_1'=4,'seq_2'=2] {'seq_0'}, dimensions={0}, use_global_device_ids=true | all-gather | bytes 276480 | tf_op jit(solution)/shard_map/all_gather | solution.py:36
  380.6 9.8 %all-gather.4 = f32[4,18,768]{2,1,0:T(8,128)S(1)} all-gather(f32[1,18,768]{2,1,0:T(8,128)S(1)} %maximum_bitcast_fusion.1), channel_id=3, replica_groups=mesh['grp'=4,'seq_0'=4,'seq_1'=4,'seq_2'=2] {'seq_1'}, dimensions={0}, use_global_device_ids=true | all-gather | bytes 276480 | tf_op jit(solution)/shard_map/all_gather | solution.py:36
  390.6 7.5 %all-gather.5 = f32[2,18,768]{2,1,0:T(8,128)S(1)} all-gather(f32[1,18,768]{2,1,0:T(8,128)S(1)} %maximum_bitcast_fusion.2), channel_id=4, replica_groups=mesh['grp'=4,'seq_0'=4,'seq_1'=4,'seq_2'=2] {'seq_2'}, dimensions={0}, use_global_device_ids=true | all-gather | bytes 165888 | tf_op jit(solution)/shard_map/all_gather | solution.py:36
  (247 shorter events, 159.7 us)
Async XLA Ops:
  0.6 20.6 %copy-start = (bf16[768,2304]{1,0:T(8,128)(2,1)S(1)}, bf16[768,2304]{1,0:T(8,128)(2,1)}, u32[]{:S(2)}) copy-start(bf16[768,2304]{1,0:T(8,128)(2,1)} %param.19) | copy-start | bytes 10616836
  0.6 4.0 copy-start.3
  5.9 14.0 %copy-start.20 = (s32[2]{0:T(128)S(1)}, s32[2]{0:T(128)}, u32[]{:S(2)}) copy-start(s32[2]{0:T(128)} %param.17) | copy-start | bytes 28
  9.1 32.2 %all-to-all-start = ((bf16[2,16,32,768]{3,1,0,2:T(8,128)(2,1)}), bf16[2,16,32,768]{3,1,0,2:T(8,128)(2,1)}, u32[]{:S(2)}, u32[]{:S(2)}) async-start(bf16[2,16,32,768]{3,1,0,2:T(8,128)(2,1)} %copy.88), calls=%async_computation | async-start | bytes 3145728 | tf_op jit(solution)/shard_map/all_to_all | solution.py:146
  48.3 74.8 %copy-start.19 = (s32[4,256]{1,0:T(4,128)S(1)}, s32[4,256]{1,0:T(4,128)}, u32[]{:S(2)}) copy-start(s32[4,256]{1,0:T(4,128)} %lt.65) | copy-start | bytes 12292
  48.3 74.9 %copy-start.21 = (s32[4]{0:T(128)S(1)}, s32[4]{0:T(128)}, u32[]{:S(2)}) copy-start(s32[4]{0:T(128)} %lt.67) | copy-start | bytes 52
  59.7 3.2 copy-start.2
  59.7 3.3 copy-start.5
  70.0 3.2 copy-start.2
  70.0 3.3 copy-start.5
  93.1 3.2 copy-start.2
  93.1 3.3 copy-start.5
  103.4 3.2 copy-start.2
  103.4 3.3 copy-start.5
  117.7 32.8 %all-to-all-start.1 = ((f32[32,1,512]{2,1,0:T(1,128)}), f32[32,1,512]{2,1,0:T(1,128)S(1)}, u32[]{:S(2)}, u32[]{:S(2)}) async-start(f32[32,1,512]{2,1,0:T(1,128)} %reshape.712), calls=%async_computation.1 | async-start | bytes 131072 | tf_op jit(solution)/shard_map/all_to_all | solution.py:162
  126.9 4.8 %copy-start.8 = (bf16[2,512,768]{2,1,0:T(8,128)(2,1)S(1)}, bf16[2,512,768]{2,1,0:T(8,128)(2,1)}, u32[]{:S(2)}) copy-start(bf16[2,512,768]{2,1,0:T(8,128)(2,1)} %get-tuple-element.265) | copy-start | bytes 4718596
  133.2 3.7 copy-start.7
  150.5 142.1 %all-to-all-start.2 = ((bf16[2,512,1,768]{3,0,2,1:T(2,128)(2,1)}), bf16[2,512,1,768]{3,0,2,1:T(2,128)(2,1)}, u32[]{:S(2)}, u32[]{:S(2)}) async-start(bf16[2,512,1,768]{3,0,2,1:T(2,128)(2,1)} %bitcast.29), calls=%async_computation.2 | async-start | bytes 3145728 | tf_op jit(solution)/shard_map/all_to_all | solution.py:159
  275.7 4.4 %copy-start.17 = (pred[2,512]{1,0:T(4,128)(4,1)S(1)}, pred[2,512]{1,0:T(4,128)(4,1)}, u32[]{:S(2)}) copy-start(pred[2,512]{1,0:T(4,128)(4,1)} %get-tuple-element.253) | copy-start | bytes 3076
  293.7 63.9 %all-to-all-start.3 = ((bf16[4,192,768]{2,1,0:T(8,128)(2,1)}), bf16[4,192,768]{2,1,0:T(8,128)(2,1)}, u32[]{:S(2)}, u32[]{:S(2)}) async-start(bf16[4,192,768]{2,1,0:T(8,128)(2,1)} %broadcast_in_dim.93), calls=%async_computation.3 | async-start | bytes 2359296 | tf_op jit(solution)/shard_map/all_to_all | solution.py:14
  304.0 3.7 copy-start.4
  304.0 3.7 copy-start.11
  307.7 10.8 %copy-start.23 = (f32[768]{0:T(1024)S(1)}, f32[768]{0:T(1024)}, u32[]{:S(2)}) copy-start(f32[768]{0:T(1024)} %param.21) | copy-start | bytes 9220
  361.5 41.5 %copy-start.1 = (bf16[768,2304]{1,0:T(8,128)(2,1)S(1)}, bf16[768,2304]{1,0:T(8,128)(2,1)}, u32[]{:S(2)}) copy-start(bf16[768,2304]{1,0:T(8,128)(2,1)} %param.19) | copy-start | bytes 10616836
  (12 other events, 19.4 us)
where the time goes:
time: 411 us; the launch traced here: 403 us
  local copies, waits for them, and re-layouts  198 us (48%)
  matrix products  111 us (27%)
  starting transfers between devices  27.9 us (7%)
  blocking collectives  27.7 us (7%)
  other arithmetic  24.3 us (6%)
  waiting for transfers between devices  12 us (3%)
    dynamic_update_slice x16, local copies, waits for them, and re-layouts, near_branch(): lax.map(step, (query, key_rows, value_rows, valid.reshape(nblocks, BLOCK)))  96.7 us
    dot_general x1, matrix products, local(): jnp.dot(act, ff_out, preferred_element_type=jnp.float32)  39.2 us
    dot_general x8, matrix products, attend(): jnp.einsum('hqk,khd->qhd', probs.astype(jnp.bfloat16), value_rows, prefer...  29.7 us
    all_gather x3, blocking collectives, gathered_once(): both, at, found = (lax.all_gather(jnp.concatenate(lines), axis), 0, {})  27.7 us
    unnamed x56, local copies, waits for them, and re-layouts  27.1 us
    dot_general x8, matrix products, attend(): jnp.einsum('qhd,khd->hqk', query, key_rows, preferred_element_type=jnp.fl...  14.8 us
    reduce_sum x8, other arithmetic, attend(): total = jnp.sum(probs, axis=-1)  12.9 us
    dynamic_slice x6, local copies, waits for them, and re-layouts, far_branch(): return lax.map(per_slide, (proj, keep))  12.2 us
  transfers between devices with their start and end apart: 4, of which 1 were waited for; matrix products, arithmetic and copies ran while one was open for 57% of the time, Pallas kernels for 0%

commit v1 on v0

v1 whole, which is shorter than its diff:
```python
import functools

import jax
import jax.numpy as jnp
from jax import lax
from jax.experimental import pallas as pl
from jax.experimental.pallas import tpu as pltpu
from jax.sharding import Mesh
from jax.sharding import PartitionSpec as P


HEADS = 16
BLOCK = 256
WIDE = 896
SEQ = ("seq_0", "seq_1", "seq_2")
F32 = jnp.float32
BF16 = jnp.bfloat16
LOG2E = 1.4426950408889634
LN2 = 0.6931471805599453


def dot(a, b):
    return jnp.dot(a, b, preferred_element_type=F32)


def dot_nt(a, b):
    return lax.dot_general(a, b, (((1,), (1,)), ((), ())), preferred_element_type=F32)


def norm_rows(x, gain):
    centre = jnp.mean(x, axis=-1, keepdims=True)
    c = x - centre
    spread = jnp.mean(c * c, axis=-1, keepdims=True)
    return c * lax.rsqrt(spread + 1e-05) * gain


def thirds(x):
    hi = x.astype(BF16).astype(F32)
    rest = x - hi
    mid = rest.astype(BF16).astype(F32)
    return hi, mid, (rest - mid).astype(BF16).astype(F32)


def attention(near, slide, here_ref, counts_ref, x_ref, gain_ref, w_ref, out_ref, nrm, qs, ks, vt, ot, lt):
    step = pl.program_id(0)
    here, count = here_ref[0], counts_ref[slide]
    rows, width = nrm.shape
    head_dim = width // HEADS
    half = HEADS // 2
    span = half * head_dim

    def place(index):
        if near:
            block, rest = index // 256, index % 256
            return here * rows + block * 256 + (rest % 8) * 32 + rest // 8
        return index * 32 + here

    @pl.when(step == 0)
    def _():
        x = x_ref[...].astype(F32)
        pos = place(lax.broadcasted_iota(jnp.int32, (rows, 1), 0))
        if near:
            x = jnp.concatenate(
                [x[:, 8 * b : 8 * b + 8].reshape(rows // 2, width) for b in range(2)], 0
            )
            first = jnp.concatenate(
                [jnp.broadcast_to(x[b * 256 : b * 256 + 1], (256, width)) for b in range(2)], 0
            )
        else:
            x = x.reshape(rows, width)
            first = jnp.broadcast_to(x[0:1], x.shape)
        x = jnp.where(pos < count, x, first)
        nrm[...] = norm_rows(x, gain_ref[...]).astype(BF16)
        qs[...] = dot(nrm[...], w_ref[...]).astype(BF16)

    @pl.when(step == 1)
    def _():
        ks[...] = dot(nrm[...], w_ref[...]).astype(BF16)

    @pl.when(step == 2)
    def _():
        v = dot(nrm[...], w_ref[...])
        live = place(lax.broadcasted_iota(jnp.int32, (1, rows), 1)) < count
        values = jnp.where(live, v.T, 0.0).astype(BF16)
        ones = jnp.where(
            lax.broadcasted_iota(jnp.int32, (16, rows), 0) == 0, jnp.where(live, 1.0, 0.0), 0.0
        ).astype(BF16)
        for h in range(HEADS):
            vt[h // half, h % half, :head_dim] = values[h * head_dim : (h + 1) * head_dim]
            vt[h // half, h % half, head_dim:] = ones
        scale = LOG2E / head_dim**0.5
        keys = BLOCK if near else rows

        def part(i, carry):
            g, t = i // 2, i % 2
            base = pl.multiple_of(g * span, 128)
            qrow = pl.multiple_of(t * 256, 256)
            krow = qrow if near else 0
            for hh in range(half):
                off = hh * head_dim
                w0 = off // 128 * 128
                wide = 128 if off + head_dim <= w0 + 128 else 256
                lane = lax.broadcasted_iota(jnp.int32, (1, wide), 1) + w0
                inside = jnp.where((lane >= off) & (lane < off + head_dim), 1.0, 0.0).astype(BF16)
                cols = pl.ds(base + w0, wide)
                kh = ks[pl.ds(krow, keys), cols] * inside
                s = dot_nt(kh, qs[pl.ds(qrow, 256), cols])
                m = jnp.max(s, axis=0, keepdims=True) * scale
                p = jnp.exp2(s * scale - m).astype(BF16)
                o = dot(vt[g, hh, :, pl.ds(krow, keys)], p)
                total = jnp.maximum(o[head_dim : head_dim + 1], 1e-30)
                ot[g, off : off + head_dim, pl.ds(qrow, 256)] = o[:head_dim] * (1.0 / total)
                lt[g, hh : hh + 1, pl.ds(qrow, 256)] = (m + jnp.log2(total)) * LN2
            return carry

        lax.fori_loop(0, 4, part, 0)
        out_ref[:, :width] = ot[...].reshape(width, rows).T.astype(out_ref.dtype)
        pieces = thirds(lt[...].reshape(HEADS, rows))
        tail = jnp.concatenate([*pieces, jnp.zeros((128 - 3 * HEADS, rows), F32)], 0)
        out_ref[:, width:] = tail.T.astype(out_ref.dtype)


def attend(near, slide, where, x, gain, weight):
    classes, _, tall, width = x.shape
    rows = classes * tall
    keys = BLOCK if near else rows
    dtype = F32 if near else BF16
    return pl.pallas_call(
        functools.partial(attention, near, slide),
        out_shape=jax.ShapeDtypeStruct((rows, WIDE), dtype),
        grid_spec=pltpu.PrefetchScalarGridSpec(
            num_scalar_prefetch=2,
            grid=(3,),
            in_specs=[
                pl.BlockSpec((classes, None, tall, width), lambda i, *_: (0, slide, 0, 0)),
                pl.BlockSpec((1, width), lambda i, *_: (0, 0)),
                pl.BlockSpec((width, width), lambda i, *_: (0, i)),
            ],
            out_specs=pl.BlockSpec((rows, WIDE), lambda i, *_: (0, 0)),
            scratch_shapes=[
                pltpu.VMEM((rows, width), BF16),
                pltpu.VMEM((rows, width), BF16),
                pltpu.VMEM((rows, width), BF16),
                pltpu.VMEM((2, HEADS // 2, width // HEADS + 16, rows), BF16),
                pltpu.VMEM((2, width // 2, rows), F32),
                pltpu.VMEM((2, HEADS // 2, rows), F32),
            ],
        ),
        cost_estimate=pl.CostEstimate(
            flops=2 * rows * width * (3 * width + 2 * keys),
            bytes_accessed=2 * 3 * width * width + 6 * rows * width,
            transcendentals=rows * keys * HEADS,
        ),
        name="near" if near else "far",
    )(*where, x, gain, weight)


def gelu(x):
    return 0.5 * x * (1.0 + lax.erf(x * 0.7071067811865476))


def post(
    slide,
    here_ref,
    counts_ref,
    grp_ref,
    x_ref,
    near_ref,
    far_ref,
    wo_ref,
    gain_ref,
    w1_ref,
    w2_ref,
    wp_ref,
    cw_ref,
    enc_ref,
    red_ref,
    encs,
    logit,
):
    step = pl.program_id(0)
    here, count = here_ref[0], counts_ref[slide]
    width = wo_ref.shape[0]
    head_dim = width // HEADS
    rows = near_ref.shape[0]
    far = far_ref[...].astype(F32).reshape(rows, WIDE)
    near = near_ref[...]
    row = lax.broadcasted_iota(jnp.int32, (256, width), 0)
    lane = lax.broadcasted_iota(jnp.int32, (256, width), 1)
    slot = row % 128
    head = slot % HEADS
    hit = (slot < 3 * HEADS) & (lane >= head * head_dim) & (lane < head * head_dim + head_dim)
    spread = jnp.where(hit, jnp.where(row < 128, 1.0, -1.0), 0.0).astype(BF16)
    parts = jnp.concatenate([near[:, width:], far[:, width:]], 1).astype(BF16)
    gap = dot(parts, spread)
    share = 1.0 / (1.0 + jnp.exp(-gap))
    mixed = (share * near[:, :width] + (1.0 - share) * far[:, :width]).astype(BF16)
    resid = x_ref[...].astype(F32).reshape(rows, width) + dot(mixed, wo_ref[...])
    n2 = norm_rows(resid, gain_ref[...]).astype(BF16)
    acc = resid
    chunk = 512
    for f in range(w1_ref.shape[1] // chunk):
        u = dot(n2, w1_ref[:, f * chunk : (f + 1) * chunk])
        acc = acc + dot(gelu(u).astype(BF16), w2_ref[f * chunk : (f + 1) * chunk, :])

    def place(index):
        return here * 512 + step * 256 + (index % 8) * 32 + index // 8

    live = place(lax.broadcasted_iota(jnp.int32, (rows, 1), 0)) < count
    enc32 = jnp.where(live, acc, 0.0).astype(BF16).astype(F32)
    enc = enc32.astype(BF16)
    enc_ref[...] = enc32.reshape(enc_ref.shape).astype(BF16)
    at = pl.multiple_of(step * rows, 256)
    encs[pl.ds(at, rows), :] = enc
    pool = [wp_ref[lax.rem(grp_ref[0] - k + 4, 4)] for k in range(4)]
    z = dot(enc, jnp.concatenate(pool, 0))
    hidden = width // 2
    gate = jnp.tanh(z[:, :hidden]) * (1.0 / (1.0 + jnp.exp(-z[:, hidden:])))
    g_hi, g_mid, g_lo = thirds(gate)
    cw = cw_ref[...]
    c_hi, c_mid, c_lo = thirds(cw)
    stack = jnp.concatenate([c_hi, c_mid, c_lo], 0).astype(BF16)
    one = dot_nt(stack, g_hi.astype(BF16))
    two = dot_nt(stack[:16], g_mid.astype(BF16))
    three = dot_nt(stack[:16], g_lo.astype(BF16))
    logits = one[0:8] + ((one[8:16] + two[0:8]) + (one[16:24] + two[8:16] + three[0:8]))
    live_t = place(lax.broadcasted_iota(jnp.int32, (1, rows), 1)) < count
    logit[:, pl.ds(at, rows)] = jnp.where(live_t, logits, -1e30)

    @pl.when(step == 1)
    def _():
        every = logit[...]
        peak = jnp.max(every, axis=1, keepdims=True)
        e = jnp.where(every > -1e29, jnp.exp(every - peak), 0.0)
        total = jnp.sum(e, axis=1, keepdims=True)
        pieces = jnp.concatenate(thirds(e), 0).astype(BF16)
        numer = dot(pieces, encs[...])
        red_ref[:, :width] = numer[0:8] + (numer[8:16] + numer[16:24])
        red_ref[:, width : width + 128] = jnp.broadcast_to(peak, (8, 128))
        red_ref[:, width + 128 :] = jnp.broadcast_to(total, (8, 128))


def finish(slide, where, x, near, back, wo, gain, w1, w2, wp, cw):
    classes, _, tall, width = x.shape
    rows = classes * tall
    hidden = w1.shape[1]
    once = pl.Buffered(1)
    return pl.pallas_call(
        functools.partial(post, slide),
        out_shape=(
            jax.ShapeDtypeStruct((classes, tall, width), BF16),
            jax.ShapeDtypeStruct((8, width + 256), F32),
        ),
        grid_spec=pltpu.PrefetchScalarGridSpec(
            num_scalar_prefetch=3,
            grid=(2,),
            in_specs=[
                pl.BlockSpec((classes, None, 8, width), lambda i, *_: (0, slide, i, 0)),
                pl.BlockSpec((rows // 2, WIDE), lambda i, *_: (i, 0)),
                pl.BlockSpec((classes, 8, WIDE), lambda i, *_: (0, i, 0)),
                pl.BlockSpec((width, width), lambda i, *_: (0, 0), pipeline_mode=once),
                pl.BlockSpec((1, width), lambda i, *_: (0, 0)),
                pl.BlockSpec((width, hidden), lambda i, *_: (0, 0), pipeline_mode=once),
                pl.BlockSpec((hidden, width), lambda i, *_: (0, 0), pipeline_mode=once),
                pl.BlockSpec((4, width // 4, width), lambda i, *_: (0, 0, 0), pipeline_mode=once),
                pl.BlockSpec((8, width // 2), lambda i, *_: (0, 0)),
            ],
            out_specs=(
                pl.BlockSpec((classes, 8, width), lambda i, *_: (0, i, 0)),
                pl.BlockSpec((8, width + 256), lambda i, *_: (0, 0)),
            ),
            scratch_shapes=[pltpu.VMEM((rows, width), BF16), pltpu.VMEM((8, rows), F32)],
        ),
        cost_estimate=pl.CostEstimate(
            flops=2 * rows * width * (2 * width + 2 * hidden),
            bytes_accessed=4 * width * (width + hidden) + 8 * rows * width,
            transcendentals=rows * hidden,
        ),
        name="post",
    )(*where, x, near, back, wo, gain, w1, w2, wp, cw)


def fold(last, *refs):
    *pieces, out_ref = refs
    width = 768
    peaks = [p[:, width : width + 128] for p in pieces]
    top = functools.reduce(jnp.maximum, peaks)
    numer, total = 0.0, 0.0
    for p, peak in zip(pieces, peaks):
        w = jnp.exp(peak - top)
        numer = numer + p[:, :width] * jnp.concatenate([w] * 6, 1)
        total = total + p[:, width + 128 :] * w
    if last:
        out_ref[...] = numer / jnp.concatenate([total] * 6, 1)
    else:
        out_ref[:, :width] = numer
        out_ref[:, width : width + 128] = top
        out_ref[:, width + 128 :] = total


def folded(pieces, last):
    rows, wide = pieces[0].shape
    return pl.pallas_call(
        functools.partial(fold, last),
        out_shape=jax.ShapeDtypeStruct((rows, 768 if last else wide), F32),
        name="fold",
    )(*pieces)


def joined(x, axes):
    for axis in axes:
        size = lax.axis_size(axis)
        pieces = [x] + [
            lax.ppermute(x, axis, [(i, (i + k) % size) for i in range(size)])
            for k in range(1, size)
        ]
        x = folded(pieces, axis == axes[-1])
    return x


def exchange(x):
    return lax.all_to_all(x, SEQ, 0, 0, tiled=True)


def layer(
    tiles,
    counts,
    ln1_gain,
    qkv_weight,
    out_weight,
    ln2_gain,
    ff_in,
    ff_out,
    pool_weight,
    class_weight,
):
    slides, rows, width = tiles.shape
    ratio = lax.axis_size(SEQ)
    here = lax.axis_index(SEQ)
    where = (here.astype(jnp.int32).reshape(1), counts)
    gain1, gain2 = ln1_gain.reshape(1, width), ln2_gain.reshape(1, width)
    mine = jnp.transpose(
        tiles.reshape(slides, rows // ratio, ratio, width), (2, 0, 1, 3)
    )
    moved = exchange(mine)
    mine_at = lax.axis_index("grp")
    quarters = [pool_weight] + [
        lax.ppermute(pool_weight, "grp", [(i, (i + k) % 4) for i in range(4)]) for k in (1, 2, 3)
    ]
    whole = jnp.stack(quarters)
    near = []
    for s in range(slides):
        near.append(attend(True, s, where, mine, gain1, qkv_weight))
    back = []
    for s in range(slides):
        far = attend(False, s, where, moved, gain1, qkv_weight)
        back.append(exchange(far.reshape(ratio, rows // ratio, WIDE)))
    encoded, partial = [], []
    for s in range(slides):
        enc, red = finish(
            s, (*where, mine_at.astype(jnp.int32).reshape(1)), mine, near[s], back[s], out_weight, gain2, ff_in, ff_out, whole,
            class_weight.T,
        )
        encoded.append(jnp.swapaxes(enc, 0, 1).reshape(rows, width))
        partial.append(red)
    pooled = joined(jnp.concatenate(partial, 0), SEQ[::-1])
    return (jnp.stack(encoded), pooled.reshape(slides, 8, width))


def solution(mesh):
    torus = Mesh(
        mesh.devices.reshape(mesh.shape["grp"], 4, 4, 2), ("grp", "seq_0", "seq_1", "seq_2")
    )
    return jax.shard_map(
        layer,
        mesh=torus,
        in_specs=(P("grp", SEQ, None), P("grp"), P(), P(), P(), P(), P(), P(), P("grp", None), P()),
        out_specs=(P("grp", SEQ, None), P("grp", None, None)),
        check_vma=False,
    )
```

time: 411 us -> 186 us (0.45); the launches traced: 403 us -> 184 us
  local copies, waits for them, and re-layouts: 198 us -> 11.8 us
  matrix products: 111 us -> 0 us
  Pallas kernels: 0 us -> 104 us
  blocking collectives: 27.7 us -> 0 us
  other arithmetic: 24.3 us -> 2.43 us
  waiting for transfers between devices: 12 us -> 29.4 us
  starting transfers between devices: 27.9 us -> 35.7 us
    dot_general x23 -> x0, matrix products: 111 us -> none  [the longest x1 39.2 us: local(): jnp.dot(act, ff_out, preferred_element_type=jnp.float32)]
    pallas_call x0 -> x9, Pallas kernels: none -> 104 us  [the longest x4 65.2 us: attend(): pl.pallas_call(functools.partial(attention, near, slide), out_shape=jax.S...]
    dynamic_update_slice x28 -> x0, local copies, waits for them, and re-layouts: 99 us -> none  [the longest x16 96.7 us: near_branch(): lax.map(step, (query, key_rows, value_rows, valid.reshape(nblocks, BLOCK)))]
    all_gather x3 -> x0, blocking collectives: 27.7 us -> none  [gathered_once(): both, at, found = (lax.all_gather(jnp.concatenate(lines), axis), 0, {})]
    unnamed x56 -> x31, local copies, waits for them, and re-layouts: 27.1 us -> 4.79 us
    reduce_sum x12 -> x0, other arithmetic: 18.3 us -> none  [the longest x8 12.9 us: attend(): total = jnp.sum(probs, axis=-1)]
    while x31 -> x0, local copies, waits for them, and re-layouts: 17 us -> none  [the longest x2 6.03 us: far_branch(): return lax.map(per_slide, (proj, keep))]
    dynamic_slice x10 -> x0, local copies, waits for them, and re-layouts: 12.3 us -> none  [the longest x6 12.2 us: far_branch(): return lax.map(per_slide, (proj, keep))]
  transfers between devices with their start and end apart: 4 -> 13, of which waited for: 1 -> 6; matrix products, arithmetic and copies ran while one was open for 57% -> 3% of each run, Pallas kernels for 0% -> 34%
where the time goes in v1:
time: 186 us; the launch traced here: 184 us
  Pallas kernels  104 us (56%)
  starting transfers between devices  35.7 us (19%)
  waiting for transfers between devices  29.4 us (16%)
  local copies, waits for them, and re-layouts  11.8 us (6%)
  other arithmetic  2.43 us (1%)
    pallas_call x4, Pallas kernels, attend(): pl.pallas_call(functools.partial(attention, near, slide), out_shape=jax.S...  65.2 us
    pallas_call x2, Pallas kernels, finish(): pl.pallas_call(functools.partial(post, slide), out_shape=(jax.ShapeDtypeS...  33.8 us
    all_to_all x3, starting transfers between devices, exchange(): return lax.all_to_all(x, SEQ, 0, 0, tiled=True)  23.6 us
    all_to_all x3, waiting for transfers between devices, exchange(): return lax.all_to_all(x, SEQ, 0, 0, tiled=True)  21.6 us
    ppermute x7, waiting for transfers between devices, joined(): lax.ppermute(x, axis, [(i, (i + k) % size) for i in range(size)])  7.82 us
    ppermute x7, starting transfers between devices, joined(): lax.ppermute(x, axis, [(i, (i + k) % size) for i in range(size)])  7.71 us
    unnamed x31, local copies, waits for them, and re-layouts  4.79 us
    pallas_call x3, Pallas kernels, folded(): pl.pallas_call(functools.partial(fold, last), out_shape=jax.ShapeDtypeStr...  4.71 us
  transfers between devices with their start and end apart: 13, of which 6 were waited for; matrix products, arithmetic and copies ran while one was open for 3% of the time, Pallas kernels for 34%

profile of v1, /device:TPU:1, one launch (start us, length us, event | category | flops | bytes accessed | tf_op | source)
XLA Modules:
  0.0 183.8 jit_solution(13368016134588757290)
XLA Ops:
  0.6 3.4 %copy.16 = bf16[2,16,32,768]{3,1,0,2:T(8,128)(2,1)} copy(bf16[2,16,32,768]{3,2,1,0:T(8,128)(2,1)} %bitcast.20) | data formatting | bytes 3145728 | tf_op jit(solution)/shard_map/reshape | solution.py:343
  4.0 9.6 %all-to-all-start = ((bf16[32,2,16,768]{3,2,1,0:T(8,128)(2,1)}), bf16[32,2,16,768]{3,2,1,0:T(8,128)(2,1)S(1)}, u32[]{:S(2)}, u32[]{:S(2)}) async-start(bf16[32,2,16,768]{3,2,1,0:T(8,128)(2,1)} %bitcast.17.x_ref), calls=%async_computation | async-start | bytes 3145728 | tf_op jit(solution)/shard_map/all_to_all | solution.py:322
  14.2 21.6 %all-to-all-done.x_ref = bf16[32,2,16,768]{3,2,1,0:T(8,128)(2,1)S(1)} async-done(((bf16[32,2,16,768]{3,2,1,0:T(8,128)(2,1)}), bf16[32,2,16,768]{3,2,1,0:T(8,128)(2,1)S(1)}, u32[]{:S(2)}, u32[]{:S(2)}) %all-to-all-start) | async-done | bytes 1572896 | tf_op jit(solution)/shard_map/all_to_all | solution.py:322
  37.0 18.8 %far.2 = bf16[512,896]{1,0:T(8,128)(2,1)} custom-call(s32[1]{0:T(128)} %bitcast.here_ref, s32[2]{0:T(128)} %counts_ref.11, bf16[32,2,16,768]{3,2,1,0:T(8,128)(2,1)} %copy-done, f32[1,768]{1,0:T(1,128)} %reshape.32.gain_ref, bf16[768,2304]{1,0:T(8,128)(2,1)} %w_ref.7), custom_call_target="tpu_custom_call" | custom-call | flops 2617245696 | bytes 5898240 | tf_op jit(solution)/shard_map/far/pallas_call | solution.py:128
  55.7 5.7 %all-to-all-start.1 = ((bf16[32,16,896]{2,1,0:T(8,128)(2,1)}), bf16[32,16,896]{2,1,0:T(8,128)(2,1)S(1)}, u32[]{:S(2)}, u32[]{:S(2)}) async-start(bf16[32,16,896]{2,1,0:T(8,128)(2,1)} %bitcast.22), calls=%async_computation.1 | async-start | bytes 1835008 | tf_op jit(solution)/shard_map/all_to_all | solution.py:322
  61.4 1.4 collective-permute-start
  62.8 1.5 collective-permute-start.2
  64.3 1.6 collective-permute-start.1
  65.9 13.8 %near.3.near_ref = f32[512,896]{1,0:T(8,128)} custom-call(s32[1]{0:T(128)} %bitcast.here_ref, s32[2]{0:T(128)} %counts_ref.11, bf16[32,2,16,768]{3,2,1,0:T(8,128)(2,1)} %bitcast.17.x_ref, f32[1,768]{1,0:T(1,128)} %reshape.32.gain_ref, bf16[768,2304]{1,0:T(8,128)(2,1)} %w_ref.7), custom_call_target="tpu_custom_call" | custom-call | flops 2214592512 | bytes 5898240 | tf_op jit(solution)/shard_map/near/pallas_call | solution.py:128
  79.6 18.8 %far.3 = bf16[512,896]{1,0:T(8,128)(2,1)} custom-call(s32[1]{0:T(128)} %bitcast.here_ref, s32[2]{0:T(128)} %counts_ref.11, bf16[32,2,16,768]{3,2,1,0:T(8,128)(2,1)} %copy-done, f32[1,768]{1,0:T(1,128)} %reshape.32.gain_ref, bf16[768,2304]{1,0:T(8,128)(2,1)} %w_ref.7), custom_call_target="tpu_custom_call" | custom-call | flops 2617245696 | bytes 5898240 | tf_op jit(solution)/shard_map/far/pallas_call | solution.py:128
  98.4 8.3 %all-to-all-start.2 = ((bf16[32,16,896]{2,1,0:T(8,128)(2,1)}), bf16[32,16,896]{2,1,0:T(8,128)(2,1)S(1)}, u32[]{:S(2)}, u32[]{:S(2)}) async-start(bf16[32,16,896]{2,1,0:T(8,128)(2,1)} %bitcast.21), calls=%async_computation.2 | async-start | bytes 1835008 | tf_op jit(solution)/shard_map/all_to_all | solution.py:322
  106.8 13.9 %near.2.near_ref = f32[512,896]{1,0:T(8,128)} custom-call(s32[1]{0:T(128)} %bitcast.here_ref, s32[2]{0:T(128)} %counts_ref.11, bf16[32,2,16,768]{3,2,1,0:T(8,128)(2,1)} %bitcast.17.x_ref, f32[1,768]{1,0:T(1,128)} %reshape.32.gain_ref, bf16[768,2304]{1,0:T(8,128)(2,1)} %w_ref.7), custom_call_target="tpu_custom_call" | custom-call | flops 2214592512 | bytes 5898240 | tf_op jit(solution)/shard_map/near/pallas_call | solution.py:128
  122.4 16.9 %post.2 = (bf16[32,16,768]{2,1,0:T(8,128)(2,1)}, f32[8,1024]{1,0:T(8,128)}) custom-call(s32[1]{0:T(128)} %bitcast.here_ref, s32[2]{0:T(128)} %counts_ref.11, s32[1]{0:T(128)} %bitcast.1.grp_ref, bf16[32,2,16,768]{3,2,1,0:T(8,128)(2,1)} %bitcast.17.x_ref, f32[512,896]{1,0:T(8,128)} %near.2.near_ref, bf16[32,16,896]{2,1,0:T(8,128)(2,1)} %copy-done.1, ...), custom_call_target="tpu_custom_call" | custom-call | flops 6039797760 | bytes 14942208 | tf_op jit(solution)/shard_map/post/pallas_call | solution.py:248
  141.0 16.9 %post.3 = (bf16[32,16,768]{2,1,0:T(8,128)(2,1)}, f32[8,1024]{1,0:T(8,128)}) custom-call(s32[1]{0:T(128)} %bitcast.here_ref, s32[2]{0:T(128)} %counts_ref.11, s32[1]{0:T(128)} %bitcast.1.grp_ref, bf16[32,2,16,768]{3,2,1,0:T(8,128)(2,1)} %bitcast.17.x_ref, f32[512,896]{1,0:T(8,128)} %near.3.near_ref, bf16[32,16,896]{2,1,0:T(8,128)(2,1)} %copy-done.2, ...), custom_call_target="tpu_custom_call" | custom-call | flops 6039797760 | bytes 14942208 | tf_op jit(solution)/shard_map/post/pallas_call | solution.py:248
  160.7 1.5 fold.3.refs_0_
  162.3 2.5 %collective-permute-start.6 = (f32[16,1024]{1,0:T(8,128)}, f32[16,1024]{1,0:T(8,128)S(1)}, u32[]{:S(2)}, u32[]{:S(2)}) collective-permute-start(f32[16,1024]{1,0:T(8,128)} %fold.3.refs_0_), channel_id=1, source_target_pairs={{0,6},{2,0},{4,2},{6,4},{1,7},{3,1},{5,3},{7,5},{8,14},{10,8},{12,... | collective-permute-start | bytes 196616 | tf_op jit(solution)/shard_map/ppermute | solution.py:314
  165.9 1.4 copy.14
  167.6 2.1 %collective-permute-done.5.refs_2_ = f32[16,1024]{1,0:T(8,128)S(1)} collective-permute-done((f32[16,1024]{1,0:T(8,128)}, f32[16,1024]{1,0:T(8,128)S(1)}, u32[]{:S(2)}, u32[]{:S(2)}) %collective-permute-start.5) | collective-permute-done | bytes 65568 | tf_op jit(solution)/shard_map/ppermute | solution.py:314
  169.6 1.7 collective-permute-done.4.refs_1_
  172.0 1.6 fold.4.refs_0_
  173.6 2.5 %collective-permute-start.9 = (f32[16,1024]{1,0:T(8,128)}, f32[16,1024]{1,0:T(8,128)S(1)}, u32[]{:S(2)}, u32[]{:S(2)}) collective-permute-start(f32[16,1024]{1,0:T(8,128)} %fold.4.refs_0_), channel_id=1, source_target_pairs={{0,24},{8,0},{16,8},{24,16},{1,25},{9,1},{17,9},{25,17},{2,26},{10... | collective-permute-start | bytes 196616 | tf_op jit(solution)/shard_map/ppermute | solution.py:314
  177.1 1.3 pad_maximum_fusion
  178.4 2.5 %collective-permute-done.8.refs_2_ = f32[16,1024]{1,0:T(8,128)S(1)} collective-permute-done((f32[16,1024]{1,0:T(8,128)}, f32[16,1024]{1,0:T(8,128)S(1)}, u32[]{:S(2)}, u32[]{:S(2)}) %collective-permute-start.8) | collective-permute-done | bytes 65568 | tf_op jit(solution)/shard_map/ppermute | solution.py:314
  182.2 1.6 fold.5
  (50 shorter events, 12.4 us)
Async XLA Ops:
  4.0 9.6 %copy-start.13 = (f32[768]{0:T(1024)S(1)}, f32[768]{0:T(1024)}, u32[]{:S(2)}) copy-start(f32[768]{0:T(1024)} %param.12) | copy-start | bytes 9220
  4.0 31.7 %all-to-all-start = ((bf16[32,2,16,768]{3,2,1,0:T(8,128)(2,1)}), bf16[32,2,16,768]{3,2,1,0:T(8,128)(2,1)S(1)}, u32[]{:S(2)}, u32[]{:S(2)}) async-start(bf16[32,2,16,768]{3,2,1,0:T(8,128)(2,1)} %bitcast.17.x_ref), calls=%async_computation | async-start | bytes 3145728 | tf_op jit(solution)/shard_map/all_to_all | solution.py:322
  35.8 1.2 copy-start
  55.7 5.7 %copy-start.4 = (bf16[192,768]{1,0:T(8,128)(2,1)S(1)}, bf16[192,768]{1,0:T(8,128)(2,1)}, u32[]{:S(2)}) copy-start(bf16[192,768]{1,0:T(8,128)(2,1)} %param.18) | copy-start | bytes 884740
  55.7 42.7 %all-to-all-start.1 = ((bf16[32,16,896]{2,1,0:T(8,128)(2,1)}), bf16[32,16,896]{2,1,0:T(8,128)(2,1)S(1)}, u32[]{:S(2)}, u32[]{:S(2)}) async-start(bf16[32,16,896]{2,1,0:T(8,128)(2,1)} %bitcast.22), calls=%async_computation.1 | async-start | bytes 1835008 | tf_op jit(solution)/shard_map/all_to_all | solution.py:322
  61.4 59.9 %collective-permute-start = (bf16[192,768]{1,0:T(8,128)(2,1)S(1)}, bf16[192,768]{1,0:T(8,128)(2,1)S(1)}, u32[]{:S(2)}, u32[]{:S(2)}) collective-permute-start(bf16[192,768]{1,0:T(8,128)(2,1)S(1)} %copy-done.4), channel_id=1, source_target_pairs={{0,32},{32,64},{64,96},{96,0},{1,33},{33,65},{65,97},{97,1},{2,34}... | collective-permute-start | bytes 884744 | tf_op jit(solution)/shard_map/ppermute | solution.py:348
  62.8 58.5 %collective-permute-start.2 = (bf16[192,768]{1,0:T(8,128)(2,1)S(1)}, bf16[192,768]{1,0:T(8,128)(2,1)S(1)}, u32[]{:S(2)}, u32[]{:S(2)}) collective-permute-start(bf16[192,768]{1,0:T(8,128)(2,1)S(1)} %copy-done.4), channel_id=1, source_target_pairs={{0,96},{32,0},{64,32},{96,64},{1,97},{33,1},{65,33},{97,65},{2,98}... | collective-permute-start | bytes 884744 | tf_op jit(solution)/shard_map/ppermute | solution.py:348
  64.3 57.0 %collective-permute-start.1 = (bf16[192,768]{1,0:T(8,128)(2,1)S(1)}, bf16[192,768]{1,0:T(8,128)(2,1)S(1)}, u32[]{:S(2)}, u32[]{:S(2)}) collective-permute-start(bf16[192,768]{1,0:T(8,128)(2,1)S(1)} %copy-done.4), channel_id=1, source_target_pairs={{0,64},{32,96},{64,0},{96,32},{1,65},{33,97},{65,1},{97,33},{2,66}... | collective-permute-start | bytes 884744 | tf_op jit(solution)/shard_map/ppermute | solution.py:348
  98.4 22.2 %copy-start.1 = (bf16[32,16,896]{2,1,0:T(8,128)(2,1)}, bf16[32,16,896]{2,1,0:T(8,128)(2,1)S(1)}, u32[]{:S(2)}) copy-start(bf16[32,16,896]{2,1,0:T(8,128)(2,1)S(1)} %all-to-all-done.1.far_ref) | copy-start | bytes 2752516
  98.4 41.6 %all-to-all-start.2 = ((bf16[32,16,896]{2,1,0:T(8,128)(2,1)}), bf16[32,16,896]{2,1,0:T(8,128)(2,1)S(1)}, u32[]{:S(2)}, u32[]{:S(2)}) async-start(bf16[32,16,896]{2,1,0:T(8,128)(2,1)} %bitcast.21), calls=%async_computation.2 | async-start | bytes 1835008 | tf_op jit(solution)/shard_map/all_to_all | solution.py:322
  106.8 13.9 %copy-start.14 = (f32[768]{0:T(1024)S(1)}, f32[768]{0:T(1024)}, u32[]{:S(2)}) copy-start(f32[768]{0:T(1024)} %param.15) | copy-start | bytes 9220
  140.1 0.9 copy-start.2
  157.9 9.4 %copy-start.3 = (bf16[32,16,768]{2,1,0:T(8,128)(2,1)S(1)}, bf16[32,16,768]{2,1,0:T(8,128)(2,1)}, u32[]{:S(2)}) copy-start(bf16[32,16,768]{2,1,0:T(8,128)(2,1)} %get-tuple-element.6) | copy-start | bytes 2359300
  158.7 1.4 copy-start.5
  158.7 1.4 collective-permute-start.3
  162.3 5.3 %collective-permute-start.6 = (f32[16,1024]{1,0:T(8,128)}, f32[16,1024]{1,0:T(8,128)S(1)}, u32[]{:S(2)}, u32[]{:S(2)}) collective-permute-start(f32[16,1024]{1,0:T(8,128)} %fold.3.refs_0_), channel_id=1, source_target_pairs={{0,6},{2,0},{4,2},{6,4},{1,7},{3,1},{5,3},{7,5},{8,14},{10,8},{12,... | collective-permute-start | bytes 196616 | tf_op jit(solution)/shard_map/ppermute | solution.py:314
  164.8 4.9 %collective-permute-start.5 = (f32[16,1024]{1,0:T(8,128)}, f32[16,1024]{1,0:T(8,128)S(1)}, u32[]{:S(2)}, u32[]{:S(2)}) collective-permute-start(f32[16,1024]{1,0:T(8,128)} %fold.3.refs_0_), channel_id=1, source_target_pairs={{0,4},{2,6},{4,0},{6,2},{1,5},{3,7},{5,1},{7,3},{8,12},{10,14},{12... | collective-permute-start | bytes 196616 | tf_op jit(solution)/shard_map/ppermute | solution.py:314
  165.3 6.0 %collective-permute-start.4 = (f32[16,1024]{1,0:T(8,128)}, f32[16,1024]{1,0:T(8,128)S(1)}, u32[]{:S(2)}, u32[]{:S(2)}) collective-permute-start(f32[16,1024]{1,0:T(8,128)} %fold.3.refs_0_), channel_id=1, source_target_pairs={{0,2},{2,4},{4,6},{6,0},{1,3},{3,5},{5,7},{7,1},{8,10},{10,12},{12... | collective-permute-start | bytes 196616 | tf_op jit(solution)/shard_map/ppermute | solution.py:314
  167.5 3.8 %copy-start.6 = (f32[16,1024]{1,0:T(8,128)}, f32[16,1024]{1,0:T(8,128)S(1)}, u32[]{:S(2)}) copy-start(f32[16,1024]{1,0:T(8,128)S(1)} %collective-permute-done.6.refs_3_) | copy-start | bytes 196612
  169.6 1.7 copy-start.7
  173.6 4.9 %collective-permute-start.9 = (f32[16,1024]{1,0:T(8,128)}, f32[16,1024]{1,0:T(8,128)S(1)}, u32[]{:S(2)}, u32[]{:S(2)}) collective-permute-start(f32[16,1024]{1,0:T(8,128)} %fold.4.refs_0_), channel_id=1, source_target_pairs={{0,24},{8,0},{16,8},{24,16},{1,25},{9,1},{17,9},{25,17},{2,26},{10... | collective-permute-start | bytes 196616 | tf_op jit(solution)/shard_map/ppermute | solution.py:314
  176.1 4.9 %collective-permute-start.8 = (f32[16,1024]{1,0:T(8,128)}, f32[16,1024]{1,0:T(8,128)S(1)}, u32[]{:S(2)}, u32[]{:S(2)}) collective-permute-start(f32[16,1024]{1,0:T(8,128)} %fold.4.refs_0_), channel_id=1, source_target_pairs={{0,16},{8,24},{16,0},{24,8},{1,17},{9,25},{17,1},{25,9},{2,18},{10... | collective-permute-start | bytes 196616 | tf_op jit(solution)/shard_map/ppermute | solution.py:314
  176.5 5.1 %collective-permute-start.7 = (f32[16,1024]{1,0:T(8,128)}, f32[16,1024]{1,0:T(8,128)S(1)}, u32[]{:S(2)}, u32[]{:S(2)}) collective-permute-start(f32[16,1024]{1,0:T(8,128)} %fold.4.refs_0_), channel_id=1, source_target_pairs={{0,8},{8,16},{16,24},{24,0},{1,9},{9,17},{17,25},{25,1},{2,10},{10... | collective-permute-start | bytes 196616 | tf_op jit(solution)/shard_map/ppermute | solution.py:314
  178.4 3.2 %copy-start.8 = (f32[16,1024]{1,0:T(8,128)}, f32[16,1024]{1,0:T(8,128)S(1)}, u32[]{:S(2)}) copy-start(f32[16,1024]{1,0:T(8,128)S(1)} %collective-permute-done.9.refs_3_) | copy-start | bytes 196612
  (4 other events, 2.6 us)

commit v2 on v1

v2 whole, which is shorter than its diff:
```python
import functools

import jax
import jax.numpy as jnp
from jax import lax
from jax.experimental import pallas as pl
from jax.experimental.pallas import tpu as pltpu
from jax.sharding import Mesh
from jax.sharding import PartitionSpec as P


HEADS = 16
BLOCK = 256
WIDE = 896
SEQ = ("seq_0", "seq_1", "seq_2")
F32 = jnp.float32
BF16 = jnp.bfloat16
LOG2E = 1.4426950408889634
LN2 = 0.6931471805599453


def dot(a, b):
    return jnp.dot(a, b, preferred_element_type=F32)


def dot_nt(a, b):
    return lax.dot_general(a, b, (((1,), (1,)), ((), ())), preferred_element_type=F32)


def norm_rows(x, gain):
    centre = jnp.mean(x, axis=-1, keepdims=True)
    c = x - centre
    spread = jnp.mean(c * c, axis=-1, keepdims=True)
    return c * lax.rsqrt(spread + 1e-05) * gain


def thirds(x):
    hi = x.astype(BF16).astype(F32)
    rest = x - hi
    mid = rest.astype(BF16).astype(F32)
    return hi, mid, (rest - mid).astype(BF16).astype(F32)


def attention(near, slide, here_ref, counts_ref, x_ref, gain_ref, w_ref, out_ref, nrm, qs, ks, vt, ot, lt, sc, mx, ps):
    step = pl.program_id(0)
    here, count = here_ref[0], counts_ref[slide]
    rows, width = nrm.shape
    head_dim = width // HEADS
    half = HEADS // 2
    span = half * head_dim

    def place(index):
        if near:
            block, rest = index // 256, index % 256
            return here * rows + block * 256 + (rest % 8) * 32 + rest // 8
        return index * 32 + here

    @pl.when(step == 0)
    def _():
        x = x_ref[...].astype(F32)
        pos = place(lax.broadcasted_iota(jnp.int32, (rows, 1), 0))
        if near:
            x = jnp.concatenate(
                [x[:, 8 * b : 8 * b + 8].reshape(rows // 2, width) for b in range(2)], 0
            )
            first = jnp.concatenate(
                [jnp.broadcast_to(x[b * 256 : b * 256 + 1], (256, width)) for b in range(2)], 0
            )
        else:
            x = x.reshape(rows, width)
            first = jnp.broadcast_to(x[0:1], x.shape)
        x = jnp.where(pos < count, x, first)
        nrm[...] = norm_rows(x, gain_ref[...]).astype(BF16)
        qs[...] = dot(nrm[...], w_ref[...]).astype(BF16)

    @pl.when(step == 1)
    def _():
        ks[...] = dot(nrm[...], w_ref[...]).astype(BF16)

    @pl.when(step == 2)
    def _():
        v = dot(nrm[...], w_ref[...])
        live = place(lax.broadcasted_iota(jnp.int32, (1, rows), 1)) < count
        values = jnp.where(live, v.T, 0.0).astype(BF16)
        ones = jnp.where(
            lax.broadcasted_iota(jnp.int32, (16, rows), 0) == 0, jnp.where(live, 1.0, 0.0), 0.0
        ).astype(BF16)
        for h in range(HEADS):
            vt[h // half, h % half, :head_dim] = values[h * head_dim : (h + 1) * head_dim]
            vt[h // half, h % half, head_dim:] = ones
        scale = LOG2E / head_dim**0.5
        keys = BLOCK if near else rows

        def corner(i):
            g, t = i // 2, i % 2
            qrow = pl.multiple_of(t * 256, 256)
            return g, pl.multiple_of(g * span, 128), qrow, qrow if near else 0

        def scores(i, hh):
            _, base, qrow, krow = corner(i)
            off = hh * head_dim
            w0 = off // 128 * 128
            wide = 128 if off + head_dim <= w0 + 128 else 256
            lane = lax.broadcasted_iota(jnp.int32, (1, wide), 1) + w0
            inside = jnp.where((lane >= off) & (lane < off + head_dim), 1.0, 0.0).astype(BF16)
            cols = pl.ds(base + w0, wide)
            kh = ks[pl.ds(krow, keys), cols] * inside
            s = dot_nt(kh, qs[pl.ds(qrow, 256), cols])
            sc[hh % 2] = s
            mx[hh % 4] = jnp.max(s, axis=0, keepdims=True) * scale

        def weights(hh):
            s = sc[hh % 2]
            ps[hh % 2] = jnp.exp2(s * scale - mx[hh % 4]).astype(BF16)

        def mix(i, hh):
            g, _, qrow, krow = corner(i)
            off = hh * head_dim
            o = dot(vt[g, hh, :, pl.ds(krow, keys)], ps[hh % 2])
            total = jnp.maximum(o[head_dim : head_dim + 1], 1e-30)
            ot[g, off : off + head_dim, pl.ds(qrow, 256)] = o[:head_dim] * (1.0 / total)
            lt[g, hh : hh + 1, pl.ds(qrow, 256)] = (mx[hh % 4] + jnp.log2(total)) * LN2

        def part(i, carry):
            for hh in range(half):
                if hh + 1 < half:
                    scores(i, hh + 1)
                else:
                    scores(lax.rem(i + 1, 4), 0)
                if hh:
                    mix(i, hh - 1)
                else:
                    mix(lax.rem(i + 3, 4), half - 1)
                weights(hh)
            return carry

        scores(0, 0)
        lax.fori_loop(0, 4, part, 0)
        mix(3, half - 1)
        out_ref[:, :width] = ot[...].reshape(width, rows).T.astype(out_ref.dtype)
        pieces = thirds(lt[...].reshape(HEADS, rows))
        tail = jnp.concatenate([*pieces, jnp.zeros((128 - 3 * HEADS, rows), F32)], 0)
        out_ref[:, width:] = tail.T.astype(out_ref.dtype)


def attend(near, slide, where, x, gain, weight):
    classes, _, tall, width = x.shape
    rows = classes * tall
    keys = BLOCK if near else rows
    dtype = F32 if near else BF16
    return pl.pallas_call(
        functools.partial(attention, near, slide),
        out_shape=pltpu.HBM((rows, WIDE), dtype),
        grid_spec=pltpu.PrefetchScalarGridSpec(
            num_scalar_prefetch=2,
            grid=(3,),
            in_specs=[
                pl.BlockSpec((classes, None, tall, width), lambda i, *_: (0, slide, 0, 0)),
                pl.BlockSpec((1, width), lambda i, *_: (0, 0)),
                pl.BlockSpec((width, width), lambda i, *_: (0, i)),
            ],
            out_specs=pl.BlockSpec((rows, WIDE), lambda i, *_: (0, 0)),
            scratch_shapes=[
                pltpu.VMEM((rows, width), BF16),
                pltpu.VMEM((rows, width), BF16),
                pltpu.VMEM((rows, width), BF16),
                pltpu.VMEM((2, HEADS // 2, width // HEADS + 16, rows), BF16),
                pltpu.VMEM((2, width // 2, rows), F32),
                pltpu.VMEM((2, HEADS // 2, rows), F32),
                pltpu.VMEM((2, keys, 256), F32),
                pltpu.VMEM((4, 1, 256), F32),
                pltpu.VMEM((2, keys, 256), BF16),
            ],
        ),
        compiler_params=pltpu.CompilerParams(vmem_limit_bytes=20 << 20),
        cost_estimate=pl.CostEstimate(
            flops=2 * rows * width * (3 * width + 2 * keys),
            bytes_accessed=2 * 3 * width * width + 6 * rows * width,
            transcendentals=rows * keys * HEADS,
        ),
        name="near" if near else "far",
    )(*where, x, gain, weight)


def gelu(x):
    return 0.5 * x * (1.0 + lax.erf(x * 0.7071067811865476))


def halves(x):
    return jnp.concatenate([x[:, 8 * b : 8 * b + 8].reshape(256, x.shape[2]) for b in range(2)], 0)


def post(slide, here_ref, counts_ref, grp_ref, *refs):
    x_ref, near_ref, far_ref, wo_ref, gain_ref, w1_ref, w2_ref, *refs = refs
    *wp_refs, cw_ref = refs[:5]
    refs = refs[5:]
    if slide:
        other_ref, *refs = refs
    enc_ref, red_ref, n2s, acc, encs, logit, w1, w2, pool, sem = refs
    step = pl.program_id(0)
    here, count = here_ref[0], counts_ref[slide]
    width = wo_ref.shape[0]
    head_dim = width // HEADS
    rows = near_ref.shape[0]
    fetch = [pltpu.make_async_copy(w1_ref, w1, sem.at[4]), pltpu.make_async_copy(w2_ref, w2, sem.at[5])] + [
        pltpu.make_async_copy(wp_refs[k], pool.at[lax.rem(grp_ref[0] - k + 4, 4)], sem.at[k])
        for k in range(4)
    ]

    @pl.when(step == 0)
    def _():
        for copy in fetch:
            copy.start()
        far = halves(far_ref[...].astype(F32))
        near = near_ref[...]
        row = lax.broadcasted_iota(jnp.int32, (256, width), 0)
        lane = lax.broadcasted_iota(jnp.int32, (256, width), 1)
        slot = row % 128
        head = slot % HEADS
        hit = (slot < 3 * HEADS) & (lane >= head * head_dim) & (lane < head * head_dim + head_dim)
        spread = jnp.where(hit, jnp.where(row < 128, 1.0, -1.0), 0.0).astype(BF16)
        parts = jnp.concatenate([near[:, width:], far[:, width:]], 1).astype(BF16)
        gap = dot(parts, spread)
        share = 1.0 / (1.0 + jnp.exp(-gap))
        mixed = (share * near[:, :width] + (1.0 - share) * far[:, :width]).astype(BF16)
        resid = halves(x_ref[...].astype(F32)) + dot(mixed, wo_ref[...])
        acc[...] = resid
        n2s[...] = norm_rows(resid, gain_ref[...]).astype(BF16)
        for copy in fetch:
            copy.wait()

    @pl.when(step > 0)
    def _():
        at = pl.multiple_of((step - 1) * 256, 256)

        def place(index):
            return here * rows + at + (index % 8) * 32 + index // 8

        n2 = n2s[pl.ds(at, 256), :]
        total = acc[pl.ds(at, 256), :]
        chunk = 512
        hidden = w1.shape[1]
        ahead = dot(n2, w1[:, :chunk])
        for f in range(hidden // chunk):
            u = ahead
            if (f + 1) * chunk < hidden:
                ahead = dot(n2, w1[:, (f + 1) * chunk : (f + 2) * chunk])
            total = total + dot(gelu(u).astype(BF16), w2[f * chunk : (f + 1) * chunk, :])
        live = place(lax.broadcasted_iota(jnp.int32, (256, 1), 0)) < count
        enc32 = jnp.where(live, total, 0.0).astype(BF16).astype(F32)
        enc = enc32.astype(BF16)
        enc_ref[...] = enc32.reshape(enc_ref.shape).astype(BF16)
        encs[pl.ds(at, 256), :] = enc
        z = dot(enc, pool[...].reshape(width, width))
        hidden = width // 2
        gate = jnp.tanh(z[:, :hidden]) * (1.0 / (1.0 + jnp.exp(-z[:, hidden:])))
        g_hi, g_mid, g_lo = thirds(gate)
        stack = jnp.concatenate(thirds(cw_ref[...]), 0).astype(BF16)
        one = dot_nt(stack, g_hi.astype(BF16))
        two = dot_nt(stack[:16], g_mid.astype(BF16))
        three = dot_nt(stack[:16], g_lo.astype(BF16))
        logits = one[0:8] + ((one[8:16] + two[0:8]) + (one[16:24] + two[8:16] + three[0:8]))
        live_t = place(lax.broadcasted_iota(jnp.int32, (1, 256), 1)) < count
        logit[:, pl.ds(at, 256)] = jnp.where(live_t, logits, -1e30)

    @pl.when(step == 2)
    def _():
        every = logit[...]
        peak = jnp.max(every, axis=1, keepdims=True)
        e = jnp.where(every > -1e29, jnp.exp(every - peak), 0.0)
        total = jnp.sum(e, axis=1, keepdims=True)
        numer = dot(jnp.concatenate(thirds(e), 0).astype(BF16), encs[...])
        numer = numer[0:8] + (numer[8:16] + numer[16:24])
        tail = jnp.zeros((8, 128), F32)
        at = lax.broadcasted_iota(jnp.int32, (8, 128), 1)
        for k, piece in enumerate((*thirds(peak), *thirds(total))):
            tail = jnp.where(at == k, piece, tail)
        mine = jnp.concatenate([numer, tail], 1)
        if slide:
            both = jnp.concatenate([other_ref[...], mine], 0).astype(BF16)
            red_ref[...] = jnp.broadcast_to(both[None], red_ref.shape)
        else:
            red_ref[...] = mine


def finish(slide, where, x, near, back, wo, gain, w1, w2, wp, cw, other=None):
    classes, _, tall, width = x.shape
    rows = classes * tall
    hidden = w1.shape[1]
    once = pl.Buffered(1)
    if slide:
        red = pltpu.HBM((classes, 16, WIDE), BF16)
    else:
        red = pltpu.HBM((8, WIDE), F32)
    extra = [pl.BlockSpec((8, WIDE), lambda i, *_: (0, 0))] if slide else []
    return pl.pallas_call(
        functools.partial(post, slide),
        out_shape=(pltpu.HBM((classes, tall, width), BF16), red),
        grid_spec=pltpu.PrefetchScalarGridSpec(
            num_scalar_prefetch=3,
            grid=(3,),
            in_specs=[
                pl.BlockSpec(
                    (classes, None, tall, width), lambda i, *_: (0, slide, 0, 0), pipeline_mode=once
                ),
                pl.BlockSpec((rows, WIDE), lambda i, *_: (0, 0), pipeline_mode=once),
                pl.BlockSpec((classes, tall, WIDE), lambda i, *_: (0, 0, 0), pipeline_mode=once),
                pl.BlockSpec((width, width), lambda i, *_: (0, 0), pipeline_mode=once),
                pl.BlockSpec((1, width), lambda i, *_: (0, 0)),
                *[pl.BlockSpec(memory_space=pltpu.HBM)] * 6,
                pl.BlockSpec((8, width // 2), lambda i, *_: (0, 0)),
                *extra,
            ],
            out_specs=(
                pl.BlockSpec((classes, 8, width), lambda i, *_: (0, jnp.maximum(i - 1, 0), 0)),
                pl.BlockSpec(red.shape, lambda i, *_: (0,) * len(red.shape)),
            ),
            scratch_shapes=[
                pltpu.VMEM((rows, width), BF16),
                pltpu.VMEM((rows, width), F32),
                pltpu.VMEM((rows, width), BF16),
                pltpu.VMEM((8, rows), F32),
                pltpu.VMEM((width, hidden), BF16),
                pltpu.VMEM((hidden, width), BF16),
                pltpu.VMEM((4, width // 4, width), BF16),
                pltpu.SemaphoreType.DMA((6,)),
            ],
        ),
        compiler_params=pltpu.CompilerParams(vmem_limit_bytes=34 << 20),
        cost_estimate=pl.CostEstimate(
            flops=2 * rows * width * (2 * width + 2 * hidden),
            bytes_accessed=4 * width * (width + hidden) + 8 * rows * width,
            transcendentals=rows * hidden,
        ),
        name="post",
    )(*where, x, near, back, wo, gain, w1, w2, *wp, cw, *([other] if slide else []))


def fold(x_ref, out_ref):
    width = out_ref.shape[1]
    tail = x_ref[:, :, width:].astype(F32)
    at = lax.broadcasted_iota(jnp.int32, tail.shape, 2)
    peak = jnp.sum(jnp.where(at < 3, tail, 0.0), axis=2, keepdims=True)
    total = jnp.sum(jnp.where((at >= 3) & (at < 6), tail, 0.0), axis=2, keepdims=True)
    w = jnp.exp(peak - jnp.max(peak, axis=0, keepdims=True))
    numer = jnp.sum(w * x_ref[:, :, :width].astype(F32), axis=0)
    out_ref[...] = numer / jnp.sum(w * total, axis=0)


def joined(x):
    rows = x.shape[1]
    return pl.pallas_call(
        fold,
        out_shape=jax.ShapeDtypeStruct((rows, x.shape[2] - 128), F32),
        compiler_params=pltpu.CompilerParams(vmem_limit_bytes=16 << 20),
        name="fold",
    )(exchange(x))


def exchange(x):
    return lax.all_to_all(x, SEQ, 0, 0, tiled=True)


def layer(
    tiles,
    counts,
    ln1_gain,
    qkv_weight,
    out_weight,
    ln2_gain,
    ff_in,
    ff_out,
    pool_weight,
    class_weight,
):
    slides, rows, width = tiles.shape
    ratio = lax.axis_size(SEQ)
    here = lax.axis_index(SEQ)
    where = (here.astype(jnp.int32).reshape(1), counts)
    gain1, gain2 = ln1_gain.reshape(1, width), ln2_gain.reshape(1, width)
    mine = jnp.transpose(
        tiles.reshape(slides, rows // ratio, ratio, width), (2, 0, 1, 3)
    )
    moved = exchange(mine)
    mine_at = lax.axis_index("grp")
    quarters = [pool_weight]
    for k in (1, 2, 3):
        quarters.append(lax.ppermute(pool_weight, "grp", [(i, (i + k) % 4) for i in range(4)]))
    whole = [pltpu.with_memory_space_constraint(q, pltpu.HBM) for q in quarters]
    qkv_weight, out_weight, ff_in, ff_out = (
        pltpu.with_memory_space_constraint(w, pltpu.HBM)
        for w in (qkv_weight, out_weight, ff_in, ff_out)
    )
    near = []
    for s in range(slides):
        out = attend(True, s, where, mine, gain1, qkv_weight)
        near.append(pltpu.with_memory_space_constraint(out, pltpu.HBM))
    back = []
    for s in range(slides):
        far = attend(False, s, where, moved, gain1, qkv_weight)
        back.append(exchange(far.reshape(ratio, rows // ratio, WIDE)))
    encoded, partial = [], []
    for s in range(slides):
        enc, red = finish(
            s, (*where, mine_at.astype(jnp.int32).reshape(1)), mine, near[s], back[s], out_weight, gain2, ff_in, ff_out, whole,
            class_weight.T, *partial,
        )
        encoded.append(jnp.swapaxes(enc, 0, 1).reshape(rows, width))
        partial.append(red if s else pltpu.with_memory_space_constraint(red, pltpu.HBM))
    pooled = joined(partial[1])
    return (jnp.stack(encoded), pooled.reshape(slides, 8, width))


def solution(mesh):
    torus = Mesh(
        mesh.devices.reshape(mesh.shape["grp"], 4, 4, 2), ("grp", "seq_0", "seq_1", "seq_2")
    )
    return jax.shard_map(
        layer,
        mesh=torus,
        in_specs=(P("grp", SEQ, None), P("grp"), P(), P(), P(), P(), P(), P(), P("grp", None), P()),
        out_specs=(P("grp", SEQ, None), P("grp", None, None)),
        check_vma=False,
    )
```

time: 186 us -> 158 us (0.85)
  Pallas kernels: 104 us -> 78.4 us
  local copies, waits for them, and re-layouts: 11.8 us -> 4.72 us
  waiting for transfers between devices: 29.4 us -> 36 us
    pallas_call x9 -> x7, Pallas kernels: 104 us -> 78.4 us  [the longest x4 47.2 us: attend(): pl.pallas_call(functools.partial(attention, near, slide), out_shape=pltpu...]
    all_to_all x3 -> x4, waiting for transfers between devices: 21.6 us -> 36 us  [exchange(): return lax.all_to_all(x, SEQ, 0, 0, tiled=True)]
    ppermute x7 -> x0, waiting for transfers between devices: 7.82 us -> none  [joined(): lax.ppermute(x, axis, [(i, (i + k) % size) for i in range(size)])]
    ppermute x7 -> x0, starting transfers between devices: 7.71 us -> none  [joined(): lax.ppermute(x, axis, [(i, (i + k) % size) for i in range(size)])]
    all_to_all x3 -> x4, starting transfers between devices: 23.6 us -> 31.1 us  [exchange(): return lax.all_to_all(x, SEQ, 0, 0, tiled=True)]
    unnamed x31 -> x18, local copies, waits for them, and re-layouts: 4.79 us -> 0.83 us
  transfers between devices with their start and end apart: 13 -> 7, of which waited for: 6 -> 2; matrix products, arithmetic and copies ran while one was open for 3% -> 1% of each run, Pallas kernels for 34% -> 31%
where the time goes in v2:
time: 158 us; the launch traced here: 157 us
  Pallas kernels  78.4 us (50%)
  starting transfers between devices  36.1 us (23%)
  waiting for transfers between devices  36 us (23%)
  local copies, waits for them, and re-layouts  4.72 us (3%)
    pallas_call x4, Pallas kernels, attend(): pl.pallas_call(functools.partial(attention, near, slide), out_shape=pltpu...  47.2 us
    all_to_all x4, waiting for transfers between devices, exchange(): return lax.all_to_all(x, SEQ, 0, 0, tiled=True)  36 us
    all_to_all x4, starting transfers between devices, exchange(): return lax.all_to_all(x, SEQ, 0, 0, tiled=True)  31.1 us
    pallas_call x2, Pallas kernels, finish(): pl.pallas_call(functools.partial(post, slide), out_shape=(pltpu.HBM((clas...  30.1 us
    ppermute x3, starting transfers between devices, layer(): lax.ppermute(pool_weight, 'grp', [(i, (i + k) % 4) for i in range(4)])  5.06 us
    reshape x1, local copies, waits for them, and re-layouts, layer(): tiles.reshape(slides, rows // ratio, ratio, width)  3.42 us
  transfers between devices with their start and end apart: 7, of which 2 were waited for; matrix products, arithmetic and copies ran while one was open for 1% of the time, Pallas kernels for 31%

profile of v2, /device:TPU:1, one launch (start us, length us, event | category | flops | bytes accessed | tf_op | source)
XLA Modules:
  0.0 157.4 jit_solution(489145996775148603)
XLA Ops:
  0.6 3.4 %copy.16 = bf16[2,16,32,768]{3,1,0,2:T(8,128)(2,1)} copy(bf16[2,16,32,768]{3,2,1,0:T(8,128)(2,1)} %bitcast.18) | data formatting | bytes 3145728 | tf_op jit(solution)/shard_map/reshape | solution.py:382
  4.0 9.6 %all-to-all-start = ((bf16[32,2,16,768]{3,2,1,0:T(8,128)(2,1)}), bf16[32,2,16,768]{3,2,1,0:T(8,128)(2,1)S(1)}, u32[]{:S(2)}, u32[]{:S(2)}) async-start(bf16[32,2,16,768]{3,2,1,0:T(8,128)(2,1)} %bitcast.13.x_ref.refs_0_), calls=%async_computation | async-start | bytes 3145728 | tf_op jit(solution)/shard_map/all_to_all | solution.py:361
  13.7 22.1 %all-to-all-done.x_ref = bf16[32,2,16,768]{3,2,1,0:T(8,128)(2,1)S(1)} async-done(((bf16[32,2,16,768]{3,2,1,0:T(8,128)(2,1)}), bf16[32,2,16,768]{3,2,1,0:T(8,128)(2,1)S(1)}, u32[]{:S(2)}, u32[]{:S(2)}) %all-to-all-start) | async-done | bytes 1572896 | tf_op jit(solution)/shard_map/all_to_all | solution.py:361
  35.8 12.7 %far.2 = bf16[512,896]{1,0:T(8,128)(2,1)} custom-call(s32[1]{0:T(128)} %bitcast.here_ref, s32[2]{0:T(128)S(1)} %copy-done.1, bf16[32,2,16,768]{3,2,1,0:T(8,128)(2,1)S(1)} %all-to-all-done.x_ref, f32[1,768]{1,0:T(1,128)S(1)} %reshape.32.gain_ref, bf16[768,2304]{1,0:T(8,128)(2,1)} %w_ref.7), custom_call_target="tpu_custom_call" | custom-call | flops 2617245696 | bytes 5898240 | tf_op jit(solution)/shard_map/far/pallas_call | solution.py:151
  48.5 5.7 %all-to-all-start.1 = ((bf16[32,16,896]{2,1,0:T(8,128)(2,1)}), bf16[32,16,896]{2,1,0:T(8,128)(2,1)S(1)}, u32[]{:S(2)}, u32[]{:S(2)}) async-start(bf16[32,16,896]{2,1,0:T(8,128)(2,1)} %bitcast.20), calls=%async_computation.1 | async-start | bytes 1835008 | tf_op jit(solution)/shard_map/all_to_all | solution.py:361
  54.2 1.4 collective-permute-start
  55.5 2.6 %collective-permute-start.1 = (bf16[192,768]{1,0:T(8,128)(2,1)S(1)}, bf16[192,768]{1,0:T(8,128)(2,1)S(1)}, u32[]{:S(2)}, u32[]{:S(2)}) collective-permute-start(bf16[192,768]{1,0:T(8,128)(2,1)S(1)} %copy-done.6), channel_id=1, source_target_pairs={{0,64},{32,96},{64,0},{96,32},{1,65},{33,97},{65,1},{97,33},{2,66}... | collective-permute-start | bytes 884744 | tf_op jit(solution)/shard_map/ppermute | solution.py:388
  58.2 1.1 collective-permute-start.2
  59.2 12.7 %far.3 = bf16[512,896]{1,0:T(8,128)(2,1)} custom-call(s32[1]{0:T(128)} %bitcast.here_ref, s32[2]{0:T(128)S(1)} %copy-done.1, bf16[32,2,16,768]{3,2,1,0:T(8,128)(2,1)S(1)} %all-to-all-done.x_ref, f32[1,768]{1,0:T(1,128)S(1)} %reshape.32.gain_ref, bf16[768,2304]{1,0:T(8,128)(2,1)} %w_ref.7), custom_call_target="tpu_custom_call" | custom-call | flops 2617245696 | bytes 5898240 | tf_op jit(solution)/shard_map/far/pallas_call | solution.py:151
  71.9 0.0 all-to-all-done.1.refs_2_
  71.9 8.3 %all-to-all-start.2 = ((bf16[32,16,896]{2,1,0:T(8,128)(2,1)}), bf16[32,16,896]{2,1,0:T(8,128)(2,1)S(1)}, u32[]{:S(2)}, u32[]{:S(2)}) async-start(bf16[32,16,896]{2,1,0:T(8,128)(2,1)} %bitcast.19), calls=%async_computation.2 | async-start | bytes 1835008 | tf_op jit(solution)/shard_map/all_to_all | solution.py:361
  80.3 0.0 copy-start.5
  80.3 10.9 %near.2.refs_1_ = f32[512,896]{1,0:T(8,128)} custom-call(s32[1]{0:T(128)} %bitcast.here_ref, s32[2]{0:T(128)S(1)} %copy-done.1, bf16[32,2,16,768]{3,2,1,0:T(8,128)(2,1)} %bitcast.13.x_ref.refs_0_, f32[1,768]{1,0:T(1,128)S(1)} %reshape.32.gain_ref, bf16[768,2304]{1,0:T(8,128)(2,1)} %w_ref.7), custom_call_target="tpu_custom_call" | custom-call | flops 2214592512 | bytes 5898240 | tf_op jit(solution)/shard_map/near/pallas_call | solution.py:151
  91.2 10.9 %near.3.refs_1_ = f32[512,896]{1,0:T(8,128)} custom-call(s32[1]{0:T(128)} %bitcast.here_ref, s32[2]{0:T(128)S(1)} %copy-done.1, bf16[32,2,16,768]{3,2,1,0:T(8,128)(2,1)} %bitcast.13.x_ref.refs_0_, f32[1,768]{1,0:T(1,128)S(1)} %reshape.32.gain_ref, bf16[768,2304]{1,0:T(8,128)(2,1)} %w_ref.7), custom_call_target="tpu_custom_call" | custom-call | flops 2214592512 | bytes 5898240 | tf_op jit(solution)/shard_map/near/pallas_call | solution.py:151
  102.2 0.7 copy-done.7
  102.9 0.1 copy-done.8
  103.0 14.8 %post.2 = (bf16[32,16,768]{2,1,0:T(8,128)(2,1)}, f32[8,896]{1,0:T(8,128)}) custom-call(s32[1]{0:T(128)} %bitcast.here_ref, s32[2]{0:T(128)S(1)} %copy-done.1, s32[1]{0:T(128)} %bitcast.1.grp_ref, bf16[32,2,16,768]{3,2,1,0:T(8,128)(2,1)} %bitcast.13.x_ref.refs_0_, f32[512,896]{1,0:T(8,128)} %near.2.refs_1_, bf16[32,16,896]{2,1,0:T(8,128)(2,1)S(1)} %all-to-all-done.1.refs_2_, ...), custom_call_target="tpu_custom_call" | custom-call | flops 6039797760 | bytes 14942208 | tf_op jit(solution)/shard_map/post/pallas_call | solution.py:296
  117.8 15.3 %post.3 = (bf16[32,16,768]{2,1,0:T(8,128)(2,1)}, bf16[32,16,896]{2,1,0:T(8,128)(2,1)}) custom-call(s32[1]{0:T(128)} %bitcast.here_ref, s32[2]{0:T(128)S(1)} %copy-done.1, s32[1]{0:T(128)} %bitcast.1.grp_ref, bf16[32,2,16,768]{3,2,1,0:T(8,128)(2,1)} %bitcast.13.x_ref.refs_0_, f32[512,896]{1,0:T(8,128)} %near.3.refs_1_, ...), custom_call_target="tpu_custom_call" | custom-call | flops 6039797760 | bytes 14942208 | tf_op jit(solution)/shard_map/post/pallas_call | solution.py:296
  133.1 7.5 %all-to-all-start.3 = ((bf16[32,16,896]{2,1,0:T(8,128)(2,1)}), bf16[32,16,896]{2,1,0:T(8,128)(2,1)S(1)}, u32[]{:S(2)}, u32[]{:S(2)}) async-start(bf16[32,16,896]{2,1,0:T(8,128)(2,1)} %get-tuple-element.9), calls=%async_computation.3 | async-start | bytes 1835008 | tf_op jit(solution)/shard_map/all_to_all | solution.py:361
  140.7 0.2 copy.14
  140.9 0.2 copy.13
  141.2 1.3 pad_maximum_fusion
  142.5 13.9 %all-to-all-done.3.x_ref = bf16[32,16,896]{2,1,0:T(8,128)(2,1)S(1)} async-done(((bf16[32,16,896]{2,1,0:T(8,128)(2,1)}), bf16[32,16,896]{2,1,0:T(8,128)(2,1)S(1)}, u32[]{:S(2)}, u32[]{:S(2)}) %all-to-all-start.3) | async-done | bytes 917536 | tf_op jit(solution)/shard_map/all_to_all | solution.py:361
  156.3 1.0 fold.1
  (21 shorter events, 0.0 us)
Async XLA Ops:
  4.0 9.6 %copy-start.4 = (f32[768]{0:T(1024)S(1)}, f32[768]{0:T(1024)}, u32[]{:S(2)}) copy-start(f32[768]{0:T(1024)} %param.12) | copy-start | bytes 9220
  4.0 31.7 %copy-start.1 = (s32[2]{0:T(128)S(1)}, s32[2]{0:T(128)}, u32[]{:S(2)}) copy-start(s32[2]{0:T(128)} %counts_ref.11) | copy-start | bytes 28
  4.0 31.7 %all-to-all-start = ((bf16[32,2,16,768]{3,2,1,0:T(8,128)(2,1)}), bf16[32,2,16,768]{3,2,1,0:T(8,128)(2,1)S(1)}, u32[]{:S(2)}, u32[]{:S(2)}) async-start(bf16[32,2,16,768]{3,2,1,0:T(8,128)(2,1)} %bitcast.13.x_ref.refs_0_), calls=%async_computation | async-start | bytes 3145728 | tf_op jit(solution)/shard_map/all_to_all | solution.py:361
  48.5 5.7 %copy-start.6 = (bf16[192,768]{1,0:T(8,128)(2,1)S(1)}, bf16[192,768]{1,0:T(8,128)(2,1)}, u32[]{:S(2)}) copy-start(bf16[192,768]{1,0:T(8,128)(2,1)} %refs_7_.3) | copy-start | bytes 884740
  48.5 23.4 %all-to-all-start.1 = ((bf16[32,16,896]{2,1,0:T(8,128)(2,1)}), bf16[32,16,896]{2,1,0:T(8,128)(2,1)S(1)}, u32[]{:S(2)}, u32[]{:S(2)}) async-start(bf16[32,16,896]{2,1,0:T(8,128)(2,1)} %bitcast.20), calls=%async_computation.1 | async-start | bytes 1835008 | tf_op jit(solution)/shard_map/all_to_all | solution.py:361
  54.2 48.0 %collective-permute-start = (bf16[192,768]{1,0:T(8,128)(2,1)S(1)}, bf16[192,768]{1,0:T(8,128)(2,1)S(1)}, u32[]{:S(2)}, u32[]{:S(2)}) collective-permute-start(bf16[192,768]{1,0:T(8,128)(2,1)S(1)} %copy-done.6), channel_id=1, source_target_pairs={{0,32},{32,64},{64,96},{96,0},{1,33},{33,65},{65,97},{97,1},{2,34}... | collective-permute-start | bytes 884744 | tf_op jit(solution)/shard_map/ppermute | solution.py:388
  55.5 46.6 %collective-permute-start.1 = (bf16[192,768]{1,0:T(8,128)(2,1)S(1)}, bf16[192,768]{1,0:T(8,128)(2,1)S(1)}, u32[]{:S(2)}, u32[]{:S(2)}) collective-permute-start(bf16[192,768]{1,0:T(8,128)(2,1)S(1)} %copy-done.6), channel_id=1, source_target_pairs={{0,64},{32,96},{64,0},{96,32},{1,65},{33,97},{65,1},{97,33},{2,66}... | collective-permute-start | bytes 884744 | tf_op jit(solution)/shard_map/ppermute | solution.py:388
  58.2 44.0 %collective-permute-start.2 = (bf16[192,768]{1,0:T(8,128)(2,1)S(1)}, bf16[192,768]{1,0:T(8,128)(2,1)}, u32[]{:S(2)}, u32[]{:S(2)}) collective-permute-start(bf16[192,768]{1,0:T(8,128)(2,1)S(1)} %copy-done.6), channel_id=1, source_target_pairs={{0,96},{32,0},{64,32},{96,64},{1,97},{33,1},{65,33},{97,65},{2,98}... | collective-permute-start | bytes 884744 | tf_op jit(solution)/shard_map/ppermute | solution.py:388
  71.9 45.9 %all-to-all-start.2 = ((bf16[32,16,896]{2,1,0:T(8,128)(2,1)}), bf16[32,16,896]{2,1,0:T(8,128)(2,1)S(1)}, u32[]{:S(2)}, u32[]{:S(2)}) async-start(bf16[32,16,896]{2,1,0:T(8,128)(2,1)} %bitcast.19), calls=%async_computation.2 | async-start | bytes 1835008 | tf_op jit(solution)/shard_map/all_to_all | solution.py:361
  80.3 10.9 %copy-start.5 = (f32[768]{0:T(1024)S(1)}, f32[768]{0:T(1024)}, u32[]{:S(2)}) copy-start(f32[768]{0:T(1024)} %param.15) | copy-start | bytes 9220
  91.2 11.8 %copy-start = (f32[384,8]{0,1:T(8,128)S(1)}, f32[384,8]{0,1:T(8,128)}, u32[]{:S(2)}) copy-start(f32[384,8]{0,1:T(8,128)} %param.19) | copy-start | bytes 36868
  102.1 0.7 copy-start.7
  102.2 0.8 copy-start.8
  133.1 7.6 %copy-start.3 = (bf16[32,16,768]{2,1,0:T(8,128)(2,1)S(1)}, bf16[32,16,768]{2,1,0:T(8,128)(2,1)}, u32[]{:S(2)}) copy-start(bf16[32,16,768]{2,1,0:T(8,128)(2,1)} %get-tuple-element.8) | copy-start | bytes 2359300
  133.1 7.8 %copy-start.2 = (bf16[32,16,768]{2,1,0:T(8,128)(2,1)S(1)}, bf16[32,16,768]{2,1,0:T(8,128)(2,1)}, u32[]{:S(2)}) copy-start(bf16[32,16,768]{2,1,0:T(8,128)(2,1)} %get-tuple-element.6) | copy-start | bytes 2359300
  133.1 23.2 %all-to-all-start.3 = ((bf16[32,16,896]{2,1,0:T(8,128)(2,1)}), bf16[32,16,896]{2,1,0:T(8,128)(2,1)S(1)}, u32[]{:S(2)}, u32[]{:S(2)}) async-start(bf16[32,16,896]{2,1,0:T(8,128)(2,1)} %get-tuple-element.9), calls=%async_computation.3 | async-start | bytes 1835008 | tf_op jit(solution)/shard_map/all_to_all | solution.py:361

commit v3 on v2

--- a/solution.py
+++ b/solution.py
@@ -147,10 +147,9 @@
     classes, _, tall, width = x.shape
     rows = classes * tall
     keys = BLOCK if near else rows
-    dtype = F32 if near else BF16
     return pl.pallas_call(
         functools.partial(attention, near, slide),
-        out_shape=pltpu.HBM((rows, WIDE), dtype),
+        out_shape=pltpu.HBM((rows, WIDE), F32 if near else BF16),
         grid_spec=pltpu.PrefetchScalarGridSpec(
             num_scalar_prefetch=2,
             grid=(3,),
@@ -190,13 +189,13 @@
     return jnp.concatenate([x[:, 8 * b : 8 * b + 8].reshape(256, x.shape[2]) for b in range(2)], 0)
 
 
-def post(slide, here_ref, counts_ref, grp_ref, *refs):
+def post(slide, here_ref, counts_ref, grp_ref, core_ref, *refs):
     x_ref, near_ref, far_ref, wo_ref, gain_ref, w1_ref, w2_ref, *refs = refs
     *wp_refs, cw_ref = refs[:5]
     refs = refs[5:]
     if slide:
         other_ref, *refs = refs
-    enc_ref, red_ref, n2s, acc, encs, logit, w1, w2, pool, sem = refs
+    enc_ref, red_ref, n2s, acc, encs, us, logit, w1, w2, pool, sem = refs
     step = pl.program_id(0)
     here, count = here_ref[0], counts_ref[slide]
     width = wo_ref.shape[0]
@@ -212,7 +211,7 @@
         for copy in fetch:
             copy.start()
         far = halves(far_ref[...].astype(F32))
-        near = near_ref[...]
+        near = near_ref[...].astype(F32)
         row = lax.broadcasted_iota(jnp.int32, (256, width), 0)
         lane = lax.broadcasted_iota(jnp.int32, (256, width), 1)
         slot = row % 128
@@ -226,8 +225,7 @@
         resid = halves(x_ref[...].astype(F32)) + dot(mixed, wo_ref[...])
         acc[...] = resid
         n2s[...] = norm_rows(resid, gain_ref[...]).astype(BF16)
-        for copy in fetch:
-            copy.wait()
+        fetch[0].wait()
 
     @pl.when(step > 0)
     def _():
@@ -240,7 +238,14 @@
         total = acc[pl.ds(at, 256), :]
         chunk = 512
         hidden = w1.shape[1]
-        ahead = dot(n2, w1[:, :chunk])
+        us[0] = dot(n2, w1[:, :chunk])
+
+        @pl.when(step == 1)
+        def _():
+            for copy in fetch[1:]:
+                copy.wait()
+
+        ahead = us[0]
         for f in range(hidden // chunk):
             u = ahead
             if (f + 1) * chunk < hidden:
@@ -271,14 +276,11 @@
         total = jnp.sum(e, axis=1, keepdims=True)
         numer = dot(jnp.concatenate(thirds(e), 0).astype(BF16), encs[...])
         numer = numer[0:8] + (numer[8:16] + numer[16:24])
-        tail = jnp.zeros((8, 128), F32)
-        at = lax.broadcasted_iota(jnp.int32, (8, 128), 1)
-        for k, piece in enumerate((*thirds(peak), *thirds(total))):
-            tail = jnp.where(at == k, piece, tail)
-        mine = jnp.concatenate([numer, tail], 1)
+        mine = packed(peak, total, numer)
         if slide:
-            both = jnp.concatenate([other_ref[...], mine], 0).astype(BF16)
-            red_ref[...] = jnp.broadcast_to(both[None], red_ref.shape)
+            other = other_ref[...]
+            red_ref[0] = jnp.where(core_ref[0] == 0, other, mine)
+            red_ref[1] = jnp.where(core_ref[0] == 0, mine, other)
         else:
             red_ref[...] = mine
 
@@ -289,7 +291,7 @@
     hidden = w1.shape[1]
     once = pl.Buffered(1)
     if slide:
-        red = pltpu.HBM((classes, 16, WIDE), BF16)
+        red = jax.ShapeDtypeStruct((2, 8, WIDE), F32)
     else:
         red = pltpu.HBM((8, WIDE), F32)
     extra = [pl.BlockSpec((8, WIDE), lambda i, *_: (0, 0))] if slide else []
@@ -297,7 +299,7 @@
         functools.partial(post, slide),
         out_shape=(pltpu.HBM((classes, tall, width), BF16), red),
         grid_spec=pltpu.PrefetchScalarGridSpec(
-            num_scalar_prefetch=3,
+            num_scalar_prefetch=4,
             grid=(3,),
             in_specs=[
                 pl.BlockSpec(
@@ -319,6 +321,7 @@
                 pltpu.VMEM((rows, width), BF16),
                 pltpu.VMEM((rows, width), F32),
                 pltpu.VMEM((rows, width), BF16),
+                pltpu.VMEM((1, 256, 512), F32),
                 pltpu.VMEM((8, rows), F32),
                 pltpu.VMEM((width, hidden), BF16),
                 pltpu.VMEM((hidden, width), BF16),
@@ -336,25 +339,62 @@
     )(*where, x, near, back, wo, gain, w1, w2, *wp, cw, *([other] if slide else []))
 
 
-def fold(x_ref, out_ref):
-    width = out_ref.shape[1]
-    tail = x_ref[:, :, width:].astype(F32)
+def merged(x):
+    width = x.shape[2] - 128
+    tail = x[:, :, width:].astype(F32)
     at = lax.broadcasted_iota(jnp.int32, tail.shape, 2)
     peak = jnp.sum(jnp.where(at < 3, tail, 0.0), axis=2, keepdims=True)
     total = jnp.sum(jnp.where((at >= 3) & (at < 6), tail, 0.0), axis=2, keepdims=True)
-    w = jnp.exp(peak - jnp.max(peak, axis=0, keepdims=True))
-    numer = jnp.sum(w * x_ref[:, :, :width].astype(F32), axis=0)
-    out_ref[...] = numer / jnp.sum(w * total, axis=0)
-
-
-def joined(x):
-    rows = x.shape[1]
-    return pl.pallas_call(
-        fold,
-        out_shape=jax.ShapeDtypeStruct((rows, x.shape[2] - 128), F32),
-        compiler_params=pltpu.CompilerParams(vmem_limit_bytes=16 << 20),
-        name="fold",
-    )(exchange(x))
+    top = jnp.max(peak, axis=0, keepdims=True)
+    w = jnp.exp(peak - top)
+    numer = jnp.sum(w * x[:, :, :width].astype(F32), axis=0)
+    return top[0], jnp.sum(w * total, axis=0), numer
+
+
+def packed(peak, total, numer):
+    tail = jnp.zeros((8, 128), F32)
+    at = lax.broadcasted_iota(jnp.int32, (8, 128), 1)
+    for k, piece in enumerate((*thirds(peak), *thirds(total))):
+        tail = jnp.where(at == k, piece, tail)
+    return jnp.concatenate([numer, tail], 1)
+
+
+def fold_some(last, *refs):
+    *pieces, out_ref = refs
+    peak, total, numer = merged(jnp.concatenate([p[...] for p in pieces], 0))
+    if last:
+        out_ref[0] = numer / total
+    else:
+        out_ref[0] = packed(peak, total, numer)
+
+
+def joined(pair, core):
+    swap = [(0, 1), (1, 0)]
+
+    def fold(pieces, last):
+        wide = WIDE - 128 if last else WIDE
+        return pl.pallas_call(
+            functools.partial(fold_some, last),
+            out_shape=jax.ShapeDtypeStruct((1, 8, wide), F32),
+            grid=(1,),
+            in_specs=[pl.BlockSpec((1, 8, WIDE), lambda i: (0, 0, 0))] * len(pieces),
+            out_specs=pl.BlockSpec((1, 8, wide), lambda i: (0, 0, 0)),
+            compiler_params=pltpu.CompilerParams(vmem_limit_bytes=8 << 20),
+            name="fold",
+        )(*pieces)
+
+    piece = fold([pair, lax.ppermute(pair[1:], SEQ[2], swap)], False)
+    for axis in SEQ[1::-1]:
+        size = lax.axis_size(axis)
+        sent = [
+            lax.ppermute(piece, axis, [(i, (i + k) % size) for i in range(size)])
+            for k in range(1, size)
+        ]
+        piece = fold([piece, *sent], axis == SEQ[0])
+    theirs = lax.ppermute(piece, SEQ[2], swap)
+    first = core == 0
+    both = [jnp.where(first, piece, theirs), jnp.where(first, theirs, piece)]
+    return jnp.concatenate(both, 0)
 
 
 def exchange(x):
@@ -383,6 +423,7 @@
     )
     moved = exchange(mine)
     mine_at = lax.axis_index("grp")
+    core = lax.axis_index(SEQ[2])
     quarters = [pool_weight]
     for k in (1, 2, 3):
         quarters.append(lax.ppermute(pool_weight, "grp", [(i, (i + k) % 4) for i in range(4)]))
@@ -402,13 +443,13 @@
     encoded, partial = [], []
     for s in range(slides):
         enc, red = finish(
-            s, (*where, mine_at.astype(jnp.int32).reshape(1)), mine, near[s], back[s], out_weight, gain2, ff_in, ff_out, whole,
+            s, (*where, mine_at.astype(jnp.int32).reshape(1), core.astype(jnp.int32).reshape(1)), mine, near[s], back[s], out_weight, gain2, ff_in, ff_out, whole,
             class_weight.T, *partial,
         )
         encoded.append(jnp.swapaxes(enc, 0, 1).reshape(rows, width))
         partial.append(red if s else pltpu.with_memory_space_constraint(red, pltpu.HBM))
-    pooled = joined(partial[1])
-    return (jnp.stack(encoded), pooled.reshape(slides, 8, width))
+    pooled = joined(partial[1], core)
+    return (jnp.stack(encoded), pooled)
 
 
 def solution(mesh):

time: 158 us -> 153 us (0.968)
  waiting for transfers between devices: 36 us -> 24.9 us
  starting transfers between devices: 36.1 us -> 42.4 us
  Pallas kernels: 78.4 us -> 76.8 us
    all_to_all x4 -> x3, waiting for transfers between devices: 36 us -> 22.1 us  [exchange(): return lax.all_to_all(x, SEQ, 0, 0, tiled=True)]
    ppermute x0 -> x8, starting transfers between devices: none -> 13.8 us  [the longest x6 9.84 us: joined(): lax.ppermute(piece, axis, [(i, (i + k) % size) for i in range(size)])]
    all_to_all x4 -> x3, starting transfers between devices: 31.1 us -> 23.6 us  [exchange(): return lax.all_to_all(x, SEQ, 0, 0, tiled=True)]
    ppermute x0 -> x8, waiting for transfers between devices: none -> 2.72 us  [the longest x6 1.87 us: joined(): lax.ppermute(piece, axis, [(i, (i + k) % size) for i in range(size)])]
  transfers between devices with their start and end apart: 7 -> 14, of which waited for: 2 -> 4; matrix products, arithmetic and copies ran while one was open for 1% -> 2% of each run, Pallas kernels for 31% -> 32%
where the time goes in v3:
time: 153 us
  Pallas kernels  76.8 us (50%)
  starting transfers between devices  42.4 us (28%)
  waiting for transfers between devices  24.9 us (16%)
  local copies, waits for them, and re-layouts  5.85 us (4%)
  other arithmetic  1.91 us (1%)
    pallas_call x4, Pallas kernels, attend(): pl.pallas_call(functools.partial(attention, near, slide), out_shape=pltpu...  47 us
    pallas_call x2, Pallas kernels, finish(): pl.pallas_call(functools.partial(post, slide), out_shape=(pltpu.HBM((clas...  29.5 us
    all_to_all x3, starting transfers between devices, exchange(): return lax.all_to_all(x, SEQ, 0, 0, tiled=True)  23.6 us
    all_to_all x3, waiting for transfers between devices, exchange(): return lax.all_to_all(x, SEQ, 0, 0, tiled=True)  22.1 us
    ppermute x6, starting transfers between devices, joined(): lax.ppermute(piece, axis, [(i, (i + k) % size) for i in range(size)])  9.84 us
    ppermute x3, starting transfers between devices, layer(): lax.ppermute(pool_weight, 'grp', [(i, (i + k) % 4) for i in range(4)])  5.05 us
    ppermute x1, starting transfers between devices, joined(): theirs = lax.ppermute(piece, SEQ[2], swap)  3.48 us
    reshape x1, local copies, waits for them, and re-layouts, layer(): tiles.reshape(slides, rows // ratio, ratio, width)  3.42 us
  transfers between devices with their start and end apart: 14, of which 4 were waited for; matrix products, arithmetic and copies ran while one was open for 2% of the time, Pallas kernels for 32%

profile of v3, /device:TPU:1, one launch (start us, length us, event | category | flops | bytes accessed | tf_op | source)
XLA Modules:
  0.0 152.7 jit_solution(2486136012130532885)
XLA Ops:
  0.6 3.4 %copy.16 = bf16[2,16,32,768]{3,1,0,2:T(8,128)(2,1)} copy(bf16[2,16,32,768]{3,2,1,0:T(8,128)(2,1)} %bitcast.18) | data formatting | bytes 3145728 | tf_op jit(solution)/shard_map/reshape | solution.py:422
  4.0 9.6 %all-to-all-start = ((bf16[32,2,16,768]{3,2,1,0:T(8,128)(2,1)}), bf16[32,2,16,768]{3,2,1,0:T(8,128)(2,1)S(1)}, u32[]{:S(2)}, u32[]{:S(2)}) async-start(bf16[32,2,16,768]{3,2,1,0:T(8,128)(2,1)} %bitcast.13.x_ref.refs_0_), calls=%async_computation | async-start | bytes 3145728 | tf_op jit(solution)/shard_map/all_to_all | solution.py:401
  13.7 22.1 %all-to-all-done.x_ref = bf16[32,2,16,768]{3,2,1,0:T(8,128)(2,1)S(1)} async-done(((bf16[32,2,16,768]{3,2,1,0:T(8,128)(2,1)}), bf16[32,2,16,768]{3,2,1,0:T(8,128)(2,1)S(1)}, u32[]{:S(2)}, u32[]{:S(2)}) %all-to-all-start) | async-done | bytes 1572896 | tf_op jit(solution)/shard_map/all_to_all | solution.py:401
  35.8 12.6 %far.2 = bf16[512,896]{1,0:T(8,128)(2,1)} custom-call(s32[1]{0:T(128)} %bitcast.here_ref, s32[2]{0:T(128)S(1)} %copy-done.1, bf16[32,2,16,768]{3,2,1,0:T(8,128)(2,1)S(1)} %all-to-all-done.x_ref, f32[1,768]{1,0:T(1,128)S(1)} %reshape.34.gain_ref, bf16[768,2304]{1,0:T(8,128)(2,1)} %w_ref.7), custom_call_target="tpu_custom_call" | custom-call | flops 2617245696 | bytes 5898240 | tf_op jit(solution)/shard_map/far/pallas_call | solution.py:150
  48.4 5.7 %all-to-all-start.1 = ((bf16[32,16,896]{2,1,0:T(8,128)(2,1)}), bf16[32,16,896]{2,1,0:T(8,128)(2,1)S(1)}, u32[]{:S(2)}, u32[]{:S(2)}) async-start(bf16[32,16,896]{2,1,0:T(8,128)(2,1)} %bitcast.20), calls=%async_computation.1 | async-start | bytes 1835008 | tf_op jit(solution)/shard_map/all_to_all | solution.py:401
  54.1 1.4 collective-permute-start
  55.4 2.6 %collective-permute-start.1 = (bf16[192,768]{1,0:T(8,128)(2,1)S(1)}, bf16[192,768]{1,0:T(8,128)(2,1)S(1)}, u32[]{:S(2)}, u32[]{:S(2)}) collective-permute-start(bf16[192,768]{1,0:T(8,128)(2,1)S(1)} %copy-done.5), channel_id=1, source_target_pairs={{0,64},{32,96},{64,0},{96,32},{1,65},{33,97},{65,1},{97,33},{2,66}... | collective-permute-start | bytes 884744 | tf_op jit(solution)/shard_map/ppermute | solution.py:429
  58.1 1.1 collective-permute-start.2
  59.1 12.6 %far.3 = bf16[512,896]{1,0:T(8,128)(2,1)} custom-call(s32[1]{0:T(128)} %bitcast.here_ref, s32[2]{0:T(128)S(1)} %copy-done.1, bf16[32,2,16,768]{3,2,1,0:T(8,128)(2,1)S(1)} %all-to-all-done.x_ref, f32[1,768]{1,0:T(1,128)S(1)} %reshape.34.gain_ref, bf16[768,2304]{1,0:T(8,128)(2,1)} %w_ref.7), custom_call_target="tpu_custom_call" | custom-call | flops 2617245696 | bytes 5898240 | tf_op jit(solution)/shard_map/far/pallas_call | solution.py:150
  71.7 8.3 %all-to-all-start.2 = ((bf16[32,16,896]{2,1,0:T(8,128)(2,1)}), bf16[32,16,896]{2,1,0:T(8,128)(2,1)S(1)}, u32[]{:S(2)}, u32[]{:S(2)}) async-start(bf16[32,16,896]{2,1,0:T(8,128)(2,1)} %bitcast.19), calls=%async_computation.2 | async-start | bytes 1835008 | tf_op jit(solution)/shard_map/all_to_all | solution.py:401
  80.1 10.9 %near.2.refs_1_ = f32[512,896]{1,0:T(8,128)} custom-call(s32[1]{0:T(128)} %bitcast.here_ref, s32[2]{0:T(128)S(1)} %copy-done.1, bf16[32,2,16,768]{3,2,1,0:T(8,128)(2,1)} %bitcast.13.x_ref.refs_0_, f32[1,768]{1,0:T(1,128)S(1)} %reshape.34.gain_ref, bf16[768,2304]{1,0:T(8,128)(2,1)} %w_ref.7), custom_call_target="tpu_custom_call" | custom-call | flops 2214592512 | bytes 5898240 | tf_op jit(solution)/shard_map/near/pallas_call | solution.py:150
  91.0 10.9 %near.3.refs_1_ = f32[512,896]{1,0:T(8,128)} custom-call(s32[1]{0:T(128)} %bitcast.here_ref, s32[2]{0:T(128)S(1)} %copy-done.1, bf16[32,2,16,768]{3,2,1,0:T(8,128)(2,1)} %bitcast.13.x_ref.refs_0_, f32[1,768]{1,0:T(1,128)S(1)} %reshape.34.gain_ref, bf16[768,2304]{1,0:T(8,128)(2,1)} %w_ref.7), custom_call_target="tpu_custom_call" | custom-call | flops 2214592512 | bytes 5898240 | tf_op jit(solution)/shard_map/near/pallas_call | solution.py:150
  102.7 14.7 %post.2 = (bf16[32,16,768]{2,1,0:T(8,128)(2,1)}, f32[8,896]{1,0:T(8,128)}) custom-call(s32[1]{0:T(128)} %bitcast.here_ref, s32[2]{0:T(128)S(1)} %copy-done.1, s32[1]{0:T(128)} %bitcast.1.grp_ref, s32[1]{0:T(128)} %bitcast.2.core_ref, bf16[32,2,16,768]{3,2,1,0:T(8,128)(2,1)} %bitcast.13.x_ref.refs_0_, f32[512,896]{1,0:T(8,128)} %near.2.refs_1_, ...), custom_call_target="tpu_custom_call" | custom-call | flops 6039797760 | bytes 14942208 | tf_op jit(solution)/shard_map/post/pallas_call | solution.py:298
  117.4 14.9 %post.3 = (bf16[32,16,768]{2,1,0:T(8,128)(2,1)}, f32[2,8,896]{2,1,0:T(8,128)S(1)}) custom-call(s32[1]{0:T(128)} %bitcast.here_ref, s32[2]{0:T(128)S(1)} %copy-done.1, s32[1]{0:T(128)} %bitcast.1.grp_ref, s32[1]{0:T(128)} %bitcast.2.core_ref, bf16[32,2,16,768]{3,2,1,0:T(8,128)(2,1)} %bitcast.13.x_ref.refs_0_, f32[512,896]{1,0:T(8,128)} %near.3.refs_1_, ...), custom_call_target="tpu_custom_call" | custom-call | flops 6039797760 | bytes 14942208 | tf_op jit(solution)/shard_map/post/pallas_call | solution.py:298
  133.7 1.4 collective-permute-start.4
  135.1 2.4 %collective-permute-start.5 = (f32[1,8,896]{2,1,0:T(8,128)S(1)}, f32[1,8,896]{2,1,0:T(8,128)S(1)}, u32[]{:S(2)}, u32[]{:S(2)}) collective-permute-start(f32[1,8,896]{2,1,0:T(8,128)S(1)} %fold.3.refs_0_), channel_id=1, source_target_pairs={{0,4},{2,6},{4,0},{6,2},{1,5},{3,7},{5,1},{7,3},{8,12},{10,14},{12... | collective-permute-start | bytes 86024 | tf_op jit(solution)/shard_map/ppermute | solution.py:390
  137.5 1.2 collective-permute-start.6
  139.4 1.1 collective-permute-done.6.refs_3_
  140.7 1.2 collective-permute-start.7
  141.9 2.5 %collective-permute-start.8 = (f32[1,8,896]{2,1,0:T(8,128)S(1)}, f32[1,8,896]{2,1,0:T(8,128)S(1)}, u32[]{:S(2)}, u32[]{:S(2)}) collective-permute-start(f32[1,8,896]{2,1,0:T(8,128)S(1)} %fold.4.refs_0_), channel_id=1, source_target_pairs={{0,16},{8,24},{16,0},{24,8},{1,17},{9,25},{17,1},{25,9},{2,18},{10... | collective-permute-start | bytes 86024 | tf_op jit(solution)/shard_map/ppermute | solution.py:390
  144.4 1.1 collective-permute-start.9
  145.5 1.4 copy.14
  147.3 3.5 %collective-permute-start.10 = (f32[1,8,768]{2,1,0:T(8,128)S(1)}, f32[1,8,768]{2,1,0:T(8,128)S(1)}, u32[]{:S(2)}, u32[]{:S(2)}) collective-permute-start(f32[1,8,768]{2,1,0:T(8,128)S(1)} %fold.5), channel_id=1, source_target_pairs={{0,1},{1,0},{2,3},{3,2},{4,5},{5,4},{6,7},{7,6},{8,9},{9,8},{10,11... | collective-permute-start | bytes 73736 | tf_op jit(solution)/shard_map/ppermute | solution.py:394
  150.8 1.3 pad_maximum_fusion
  (38 shorter events, 4.1 us)
Async XLA Ops:
  4.0 9.6 %copy-start.3 = (f32[768]{0:T(1024)S(1)}, f32[768]{0:T(1024)}, u32[]{:S(2)}) copy-start(f32[768]{0:T(1024)} %param.12) | copy-start | bytes 9220
  4.0 31.7 %copy-start.1 = (s32[2]{0:T(128)S(1)}, s32[2]{0:T(128)}, u32[]{:S(2)}) copy-start(s32[2]{0:T(128)} %counts_ref.11) | copy-start | bytes 28
  4.0 31.7 %all-to-all-start = ((bf16[32,2,16,768]{3,2,1,0:T(8,128)(2,1)}), bf16[32,2,16,768]{3,2,1,0:T(8,128)(2,1)S(1)}, u32[]{:S(2)}, u32[]{:S(2)}) async-start(bf16[32,2,16,768]{3,2,1,0:T(8,128)(2,1)} %bitcast.13.x_ref.refs_0_), calls=%async_computation | async-start | bytes 3145728 | tf_op jit(solution)/shard_map/all_to_all | solution.py:401
  48.4 5.7 %copy-start.5 = (bf16[192,768]{1,0:T(8,128)(2,1)S(1)}, bf16[192,768]{1,0:T(8,128)(2,1)}, u32[]{:S(2)}) copy-start(bf16[192,768]{1,0:T(8,128)(2,1)} %refs_7_.3) | copy-start | bytes 884740
  48.4 23.3 %all-to-all-start.1 = ((bf16[32,16,896]{2,1,0:T(8,128)(2,1)}), bf16[32,16,896]{2,1,0:T(8,128)(2,1)S(1)}, u32[]{:S(2)}, u32[]{:S(2)}) async-start(bf16[32,16,896]{2,1,0:T(8,128)(2,1)} %bitcast.20), calls=%async_computation.1 | async-start | bytes 1835008 | tf_op jit(solution)/shard_map/all_to_all | solution.py:401
  54.1 47.8 %collective-permute-start = (bf16[192,768]{1,0:T(8,128)(2,1)S(1)}, bf16[192,768]{1,0:T(8,128)(2,1)S(1)}, u32[]{:S(2)}, u32[]{:S(2)}) collective-permute-start(bf16[192,768]{1,0:T(8,128)(2,1)S(1)} %copy-done.5), channel_id=1, source_target_pairs={{0,32},{32,64},{64,96},{96,0},{1,33},{33,65},{65,97},{97,1},{2,34}... | collective-permute-start | bytes 884744 | tf_op jit(solution)/shard_map/ppermute | solution.py:429
  55.4 46.4 %collective-permute-start.1 = (bf16[192,768]{1,0:T(8,128)(2,1)S(1)}, bf16[192,768]{1,0:T(8,128)(2,1)S(1)}, u32[]{:S(2)}, u32[]{:S(2)}) collective-permute-start(bf16[192,768]{1,0:T(8,128)(2,1)S(1)} %copy-done.5), channel_id=1, source_target_pairs={{0,64},{32,96},{64,0},{96,32},{1,65},{33,97},{65,1},{97,33},{2,66}... | collective-permute-start | bytes 884744 | tf_op jit(solution)/shard_map/ppermute | solution.py:429
  58.1 43.8 %collective-permute-start.2 = (bf16[192,768]{1,0:T(8,128)(2,1)S(1)}, bf16[192,768]{1,0:T(8,128)(2,1)}, u32[]{:S(2)}, u32[]{:S(2)}) collective-permute-start(bf16[192,768]{1,0:T(8,128)(2,1)S(1)} %copy-done.5), channel_id=1, source_target_pairs={{0,96},{32,0},{64,32},{96,64},{1,97},{33,1},{65,33},{97,65},{2,98}... | collective-permute-start | bytes 884744 | tf_op jit(solution)/shard_map/ppermute | solution.py:429
  71.7 45.7 %all-to-all-start.2 = ((bf16[32,16,896]{2,1,0:T(8,128)(2,1)}), bf16[32,16,896]{2,1,0:T(8,128)(2,1)S(1)}, u32[]{:S(2)}, u32[]{:S(2)}) async-start(bf16[32,16,896]{2,1,0:T(8,128)(2,1)} %bitcast.19), calls=%async_computation.2 | async-start | bytes 1835008 | tf_op jit(solution)/shard_map/all_to_all | solution.py:401
  80.1 10.9 %copy-start.4 = (f32[768]{0:T(1024)S(1)}, f32[768]{0:T(1024)}, u32[]{:S(2)}) copy-start(f32[768]{0:T(1024)} %param.15) | copy-start | bytes 9220
  91.0 11.8 %copy-start = (f32[384,8]{0,1:T(8,128)S(1)}, f32[384,8]{0,1:T(8,128)}, u32[]{:S(2)}) copy-start(f32[384,8]{0,1:T(8,128)} %param.19) | copy-start | bytes 36868
  101.9 0.7 copy-start.6
  101.9 0.8 copy-start.7
  132.3 14.6 %copy-start.2 = (bf16[32,16,768]{2,1,0:T(8,128)(2,1)S(1)}, bf16[32,16,768]{2,1,0:T(8,128)(2,1)}, u32[]{:S(2)}) copy-start(bf16[32,16,768]{2,1,0:T(8,128)(2,1)} %get-tuple-element.6) | copy-start | bytes 2359300
  132.3 1.3 collective-permute-start.3
  133.7 5.0 %collective-permute-start.4 = (f32[1,8,896]{2,1,0:T(8,128)S(1)}, f32[1,8,896]{2,1,0:T(8,128)S(1)}, u32[]{:S(2)}, u32[]{:S(2)}) collective-permute-start(f32[1,8,896]{2,1,0:T(8,128)S(1)} %fold.3.refs_0_), channel_id=1, source_target_pairs={{0,2},{2,4},{4,6},{6,0},{1,3},{3,5},{5,7},{7,1},{8,10},{10,12},{12... | collective-permute-start | bytes 86024 | tf_op jit(solution)/shard_map/ppermute | solution.py:390
  135.1 4.3 %collective-permute-start.5 = (f32[1,8,896]{2,1,0:T(8,128)S(1)}, f32[1,8,896]{2,1,0:T(8,128)S(1)}, u32[]{:S(2)}, u32[]{:S(2)}) collective-permute-start(f32[1,8,896]{2,1,0:T(8,128)S(1)} %fold.3.refs_0_), channel_id=1, source_target_pairs={{0,4},{2,6},{4,0},{6,2},{1,5},{3,7},{5,1},{7,3},{8,12},{10,14},{12... | collective-permute-start | bytes 86024 | tf_op jit(solution)/shard_map/ppermute | solution.py:390
  137.5 3.0 %collective-permute-start.6 = (f32[1,8,896]{2,1,0:T(8,128)S(1)}, f32[1,8,896]{2,1,0:T(8,128)S(1)}, u32[]{:S(2)}, u32[]{:S(2)}) collective-permute-start(f32[1,8,896]{2,1,0:T(8,128)S(1)} %fold.3.refs_0_), channel_id=1, source_target_pairs={{0,6},{2,0},{4,2},{6,4},{1,7},{3,1},{5,3},{7,5},{8,14},{10,8},{12,... | collective-permute-start | bytes 86024 | tf_op jit(solution)/shard_map/ppermute | solution.py:390
  140.7 6.5 %collective-permute-start.7 = (f32[1,8,896]{2,1,0:T(8,128)S(1)}, f32[1,8,896]{2,1,0:T(8,128)S(1)}, u32[]{:S(2)}, u32[]{:S(2)}) collective-permute-start(f32[1,8,896]{2,1,0:T(8,128)S(1)} %fold.4.refs_0_), channel_id=1, source_target_pairs={{0,8},{8,16},{16,24},{24,0},{1,9},{9,17},{17,25},{25,1},{2,10},{10... | collective-permute-start | bytes 86024 | tf_op jit(solution)/shard_map/ppermute | solution.py:390
  141.9 5.2 %collective-permute-start.8 = (f32[1,8,896]{2,1,0:T(8,128)S(1)}, f32[1,8,896]{2,1,0:T(8,128)S(1)}, u32[]{:S(2)}, u32[]{:S(2)}) collective-permute-start(f32[1,8,896]{2,1,0:T(8,128)S(1)} %fold.4.refs_0_), channel_id=1, source_target_pairs={{0,16},{8,24},{16,0},{24,8},{1,17},{9,25},{17,1},{25,9},{2,18},{10... | collective-permute-start | bytes 86024 | tf_op jit(solution)/shard_map/ppermute | solution.py:390
  144.4 2.8 %collective-permute-start.9 = (f32[1,8,896]{2,1,0:T(8,128)S(1)}, f32[1,8,896]{2,1,0:T(8,128)S(1)}, u32[]{:S(2)}, u32[]{:S(2)}) collective-permute-start(f32[1,8,896]{2,1,0:T(8,128)S(1)} %fold.4.refs_0_), channel_id=1, source_target_pairs={{0,24},{8,0},{16,8},{24,16},{1,25},{9,1},{17,9},{25,17},{2,26},{10... | collective-permute-start | bytes 86024 | tf_op jit(solution)/shard_map/ppermute | solution.py:390
  147.3 4.8 %collective-permute-start.10 = (f32[1,8,768]{2,1,0:T(8,128)S(1)}, f32[1,8,768]{2,1,0:T(8,128)S(1)}, u32[]{:S(2)}, u32[]{:S(2)}) collective-permute-start(f32[1,8,768]{2,1,0:T(8,128)S(1)} %fold.5), channel_id=1, source_target_pairs={{0,1},{1,0},{2,3},{3,2},{4,5},{5,4},{6,7},{7,6},{8,9},{9,8},{10,11... | collective-permute-start | bytes 73736 | tf_op jit(solution)/shard_map/ppermute | solution.py:394

commit v4 on v3

--- a/solution.py
+++ b/solution.py
@@ -70,8 +70,9 @@
             x = x.reshape(rows, width)
             first = jnp.broadcast_to(x[0:1], x.shape)
         x = jnp.where(pos < count, x, first)
-        nrm[...] = norm_rows(x, gain_ref[...]).astype(BF16)
-        qs[...] = dot(nrm[...], w_ref[...]).astype(BF16)
+        for part in (slice(0, rows // 2), slice(rows // 2, rows)):
+            nrm[part] = norm_rows(x[part], gain_ref[...]).astype(BF16)
+            qs[part] = dot(nrm[part], w_ref[...]).astype(BF16)
 
     @pl.when(step == 1)
     def _():
@@ -185,10 +186,6 @@
     return 0.5 * x * (1.0 + lax.erf(x * 0.7071067811865476))
 
 
-def halves(x):
-    return jnp.concatenate([x[:, 8 * b : 8 * b + 8].reshape(256, x.shape[2]) for b in range(2)], 0)
-
-
 def post(slide, here_ref, counts_ref, grp_ref, core_ref, *refs):
     x_ref, near_ref, far_ref, wo_ref, gain_ref, w1_ref, w2_ref, *refs = refs
     *wp_refs, cw_ref = refs[:5]
@@ -200,7 +197,7 @@
     here, count = here_ref[0], counts_ref[slide]
     width = wo_ref.shape[0]
     head_dim = width // HEADS
-    rows = near_ref.shape[0]
+    rows = acc.shape[0]
     fetch = [pltpu.make_async_copy(w1_ref, w1, sem.at[4]), pltpu.make_async_copy(w2_ref, w2, sem.at[5])] + [
         pltpu.make_async_copy(wp_refs[k], pool.at[lax.rem(grp_ref[0] - k + 4, 4)], sem.at[k])
         for k in range(4)
@@ -210,26 +207,32 @@
     def _():
         for copy in fetch:
             copy.start()
-        far = halves(far_ref[...].astype(F32))
-        near = near_ref[...].astype(F32)
-        row = lax.broadcasted_iota(jnp.int32, (256, width), 0)
-        lane = lax.broadcasted_iota(jnp.int32, (256, width), 1)
-        slot = row % 128
-        head = slot % HEADS
-        hit = (slot < 3 * HEADS) & (lane >= head * head_dim) & (lane < head * head_dim + head_dim)
-        spread = jnp.where(hit, jnp.where(row < 128, 1.0, -1.0), 0.0).astype(BF16)
+
+    @pl.when(step < 2)
+    def _():
+        head = lax.broadcasted_iota(jnp.int32, (HEADS, width), 0) * head_dim
+        lane = lax.broadcasted_iota(jnp.int32, (HEADS, width), 1)
+        hit = jnp.where((lane >= head) & (lane < head + head_dim), 1.0, 0.0)
+        rest = jnp.zeros((128 - 3 * HEADS, width), F32)
+        spread = jnp.concatenate([hit, hit, hit, rest, -hit, -hit, -hit, rest], 0).astype(BF16)
+        at = pl.ds(pl.multiple_of(step * 256, 256), 256)
+        far = far_ref[...].astype(F32).reshape(256, WIDE)
+        near = near_ref[...]
         parts = jnp.concatenate([near[:, width:], far[:, width:]], 1).astype(BF16)
         gap = dot(parts, spread)
         share = 1.0 / (1.0 + jnp.exp(-gap))
         mixed = (share * near[:, :width] + (1.0 - share) * far[:, :width]).astype(BF16)
-        resid = halves(x_ref[...].astype(F32)) + dot(mixed, wo_ref[...])
-        acc[...] = resid
-        n2s[...] = norm_rows(resid, gain_ref[...]).astype(BF16)
+        resid = x_ref[...].astype(F32).reshape(256, width) + dot(mixed, wo_ref[...])
+        acc[at, :] = resid
+        n2s[at, :] = norm_rows(resid, gain_ref[...]).astype(BF16)
+
+    @pl.when(step == 1)
+    def _():
         fetch[0].wait()
 
-    @pl.when(step > 0)
-    def _():
-        at = pl.multiple_of((step - 1) * 256, 256)
+    @pl.when(step > 1)
+    def _():
+        at = pl.multiple_of((step - 2) * 256, 256)
 
         def place(index):
             return here * rows + at + (index % 8) * 32 + index // 8
@@ -240,7 +243,7 @@
         hidden = w1.shape[1]
         us[0] = dot(n2, w1[:, :chunk])
 
-        @pl.when(step == 1)
+        @pl.when(step == 2)
         def _():
             for copy in fetch[1:]:
                 copy.wait()
@@ -268,7 +271,7 @@
         live_t = place(lax.broadcasted_iota(jnp.int32, (1, 256), 1)) < count
         logit[:, pl.ds(at, 256)] = jnp.where(live_t, logits, -1e30)
 
-    @pl.when(step == 2)
+    @pl.when(step == 3)
     def _():
         every = logit[...]
         peak = jnp.max(every, axis=1, keepdims=True)
@@ -300,13 +303,13 @@
         out_shape=(pltpu.HBM((classes, tall, width), BF16), red),
         grid_spec=pltpu.PrefetchScalarGridSpec(
             num_scalar_prefetch=4,
-            grid=(3,),
+            grid=(4,),
             in_specs=[
                 pl.BlockSpec(
-                    (classes, None, tall, width), lambda i, *_: (0, slide, 0, 0), pipeline_mode=once
+                    (classes, None, 8, width), lambda i, *_: (0, slide, jnp.minimum(i, 1), 0)
                 ),
-                pl.BlockSpec((rows, WIDE), lambda i, *_: (0, 0), pipeline_mode=once),
-                pl.BlockSpec((classes, tall, WIDE), lambda i, *_: (0, 0, 0), pipeline_mode=once),
+                pl.BlockSpec((rows // 2, WIDE), lambda i, *_: (jnp.minimum(i, 1), 0)),
+                pl.BlockSpec((classes, 8, WIDE), lambda i, *_: (0, jnp.minimum(i, 1), 0)),
                 pl.BlockSpec((width, width), lambda i, *_: (0, 0), pipeline_mode=once),
                 pl.BlockSpec((1, width), lambda i, *_: (0, 0)),
                 *[pl.BlockSpec(memory_space=pltpu.HBM)] * 6,
@@ -314,7 +317,7 @@
                 *extra,
             ],
             out_specs=(
-                pl.BlockSpec((classes, 8, width), lambda i, *_: (0, jnp.maximum(i - 1, 0), 0)),
+                pl.BlockSpec((classes, 8, width), lambda i, *_: (0, jnp.maximum(i - 2, 0), 0)),
                 pl.BlockSpec(red.shape, lambda i, *_: (0,) * len(red.shape)),
             ),
             scratch_shapes=[

time: 153 us -> 152 us (level)
  no operation moved by 1% of the time
where the time goes in v4:
time: 152 us
  Pallas kernels  75.8 us (50%)
  starting transfers between devices  42.4 us (28%)
  waiting for transfers between devices  24.9 us (16%)
  local copies, waits for them, and re-layouts  5.85 us (4%)
  other arithmetic  1.91 us (1%)
    pallas_call x4, Pallas kernels, attend(): pl.pallas_call(functools.partial(attention, near, slide), out_shape=pltpu...  46.7 us
    pallas_call x2, Pallas kernels, finish(): pl.pallas_call(functools.partial(post, slide), out_shape=(pltpu.HBM((clas...  28.8 us
    all_to_all x3, starting transfers between devices, exchange(): return lax.all_to_all(x, SEQ, 0, 0, tiled=True)  23.6 us
    all_to_all x3, waiting for transfers between devices, exchange(): return lax.all_to_all(x, SEQ, 0, 0, tiled=True)  22.1 us
    ppermute x6, starting transfers between devices, joined(): lax.ppermute(piece, axis, [(i, (i + k) % size) for i in range(size)])  9.84 us
    ppermute x3, starting transfers between devices, layer(): lax.ppermute(pool_weight, 'grp', [(i, (i + k) % 4) for i in range(4)])  5.05 us
    ppermute x1, starting transfers between devices, joined(): theirs = lax.ppermute(piece, SEQ[2], swap)  3.48 us
    reshape x1, local copies, waits for them, and re-layouts, layer(): tiles.reshape(slides, rows // ratio, ratio, width)  3.42 us
  transfers between devices with their start and end apart: 14, of which 4 were waited for; matrix products, arithmetic and copies ran while one was open for 2% of the time, Pallas kernels for 32%

profile of v4, /device:TPU:1, one launch (start us, length us, event | category | flops | bytes accessed | tf_op | source)
XLA Modules:
  0.0 151.7 jit_solution(6454201079416887900)
XLA Ops:
  0.6 3.4 %copy.16 = bf16[2,16,32,768]{3,1,0,2:T(8,128)(2,1)} copy(bf16[2,16,32,768]{3,2,1,0:T(8,128)(2,1)} %bitcast.18) | data formatting | bytes 3145728 | tf_op jit(solution)/shard_map/reshape | solution.py:425
  4.0 9.6 %all-to-all-start = ((bf16[32,2,16,768]{3,2,1,0:T(8,128)(2,1)}), bf16[32,2,16,768]{3,2,1,0:T(8,128)(2,1)S(1)}, u32[]{:S(2)}, u32[]{:S(2)}) async-start(bf16[32,2,16,768]{3,2,1,0:T(8,128)(2,1)} %bitcast.13.x_ref.refs_0_), calls=%async_computation | async-start | bytes 3145728 | tf_op jit(solution)/shard_map/all_to_all | solution.py:404
  13.7 22.1 %all-to-all-done.x_ref = bf16[32,2,16,768]{3,2,1,0:T(8,128)(2,1)S(1)} async-done(((bf16[32,2,16,768]{3,2,1,0:T(8,128)(2,1)}), bf16[32,2,16,768]{3,2,1,0:T(8,128)(2,1)S(1)}, u32[]{:S(2)}, u32[]{:S(2)}) %all-to-all-start) | async-done | bytes 1572896 | tf_op jit(solution)/shard_map/all_to_all | solution.py:404
  35.8 12.5 %far.2 = bf16[512,896]{1,0:T(8,128)(2,1)} custom-call(s32[1]{0:T(128)} %bitcast.here_ref, s32[2]{0:T(128)S(1)} %copy-done.1, bf16[32,2,16,768]{3,2,1,0:T(8,128)(2,1)S(1)} %all-to-all-done.x_ref, f32[1,768]{1,0:T(1,128)S(1)} %reshape.34.gain_ref, bf16[768,2304]{1,0:T(8,128)(2,1)} %w_ref.7), custom_call_target="tpu_custom_call" | custom-call | flops 2617245696 | bytes 5898240 | tf_op jit(solution)/shard_map/far/pallas_call | solution.py:151
  48.3 5.7 %all-to-all-start.1 = ((bf16[32,16,896]{2,1,0:T(8,128)(2,1)}), bf16[32,16,896]{2,1,0:T(8,128)(2,1)S(1)}, u32[]{:S(2)}, u32[]{:S(2)}) async-start(bf16[32,16,896]{2,1,0:T(8,128)(2,1)} %bitcast.20), calls=%async_computation.1 | async-start | bytes 1835008 | tf_op jit(solution)/shard_map/all_to_all | solution.py:404
  54.0 1.4 collective-permute-start
  55.4 2.6 %collective-permute-start.1 = (bf16[192,768]{1,0:T(8,128)(2,1)S(1)}, bf16[192,768]{1,0:T(8,128)(2,1)S(1)}, u32[]{:S(2)}, u32[]{:S(2)}) collective-permute-start(bf16[192,768]{1,0:T(8,128)(2,1)S(1)} %copy-done.5), channel_id=1, source_target_pairs={{0,64},{32,96},{64,0},{96,32},{1,65},{33,97},{65,1},{97,33},{2,66}... | collective-permute-start | bytes 884744 | tf_op jit(solution)/shard_map/ppermute | solution.py:432
  58.0 1.1 collective-permute-start.2
  59.1 12.5 %far.3 = bf16[512,896]{1,0:T(8,128)(2,1)} custom-call(s32[1]{0:T(128)} %bitcast.here_ref, s32[2]{0:T(128)S(1)} %copy-done.1, bf16[32,2,16,768]{3,2,1,0:T(8,128)(2,1)S(1)} %all-to-all-done.x_ref, f32[1,768]{1,0:T(1,128)S(1)} %reshape.34.gain_ref, bf16[768,2304]{1,0:T(8,128)(2,1)} %w_ref.7), custom_call_target="tpu_custom_call" | custom-call | flops 2617245696 | bytes 5898240 | tf_op jit(solution)/shard_map/far/pallas_call | solution.py:151
  71.6 8.3 %all-to-all-start.2 = ((bf16[32,16,896]{2,1,0:T(8,128)(2,1)}), bf16[32,16,896]{2,1,0:T(8,128)(2,1)S(1)}, u32[]{:S(2)}, u32[]{:S(2)}) async-start(bf16[32,16,896]{2,1,0:T(8,128)(2,1)} %bitcast.19), calls=%async_computation.2 | async-start | bytes 1835008 | tf_op jit(solution)/shard_map/all_to_all | solution.py:404
  80.0 10.8 %near.2.refs_1_ = f32[512,896]{1,0:T(8,128)} custom-call(s32[1]{0:T(128)} %bitcast.here_ref, s32[2]{0:T(128)S(1)} %copy-done.1, bf16[32,2,16,768]{3,2,1,0:T(8,128)(2,1)} %bitcast.13.x_ref.refs_0_, f32[1,768]{1,0:T(1,128)S(1)} %reshape.34.gain_ref, bf16[768,2304]{1,0:T(8,128)(2,1)} %w_ref.7), custom_call_target="tpu_custom_call" | custom-call | flops 2214592512 | bytes 5898240 | tf_op jit(solution)/shard_map/near/pallas_call | solution.py:151
  90.8 10.8 %near.3.refs_1_ = f32[512,896]{1,0:T(8,128)} custom-call(s32[1]{0:T(128)} %bitcast.here_ref, s32[2]{0:T(128)S(1)} %copy-done.1, bf16[32,2,16,768]{3,2,1,0:T(8,128)(2,1)} %bitcast.13.x_ref.refs_0_, f32[1,768]{1,0:T(1,128)S(1)} %reshape.34.gain_ref, bf16[768,2304]{1,0:T(8,128)(2,1)} %w_ref.7), custom_call_target="tpu_custom_call" | custom-call | flops 2214592512 | bytes 5898240 | tf_op jit(solution)/shard_map/near/pallas_call | solution.py:151
  102.4 14.3 %post.2 = (bf16[32,16,768]{2,1,0:T(8,128)(2,1)}, f32[8,896]{1,0:T(8,128)}) custom-call(s32[1]{0:T(128)} %bitcast.here_ref, s32[2]{0:T(128)S(1)} %copy-done.1, s32[1]{0:T(128)} %bitcast.1.grp_ref, s32[1]{0:T(128)} %bitcast.2.core_ref, bf16[32,2,16,768]{3,2,1,0:T(8,128)(2,1)} %bitcast.13.x_ref.refs_0_, f32[512,896]{1,0:T(8,128)} %near.2.refs_1_, ...), custom_call_target="tpu_custom_call" | custom-call | flops 6039797760 | bytes 14942208 | tf_op jit(solution)/shard_map/post/pallas_call | solution.py:301
  116.8 14.5 %post.3 = (bf16[32,16,768]{2,1,0:T(8,128)(2,1)}, f32[2,8,896]{2,1,0:T(8,128)S(1)}) custom-call(s32[1]{0:T(128)} %bitcast.here_ref, s32[2]{0:T(128)S(1)} %copy-done.1, s32[1]{0:T(128)} %bitcast.1.grp_ref, s32[1]{0:T(128)} %bitcast.2.core_ref, bf16[32,2,16,768]{3,2,1,0:T(8,128)(2,1)} %bitcast.13.x_ref.refs_0_, f32[512,896]{1,0:T(8,128)} %near.3.refs_1_, ...), custom_call_target="tpu_custom_call" | custom-call | flops 6039797760 | bytes 14942208 | tf_op jit(solution)/shard_map/post/pallas_call | solution.py:301
  132.8 1.4 collective-permute-start.4
  134.2 2.4 %collective-permute-start.5 = (f32[1,8,896]{2,1,0:T(8,128)S(1)}, f32[1,8,896]{2,1,0:T(8,128)S(1)}, u32[]{:S(2)}, u32[]{:S(2)}) collective-permute-start(f32[1,8,896]{2,1,0:T(8,128)S(1)} %fold.3.refs_0_), channel_id=1, source_target_pairs={{0,4},{2,6},{4,0},{6,2},{1,5},{3,7},{5,1},{7,3},{8,12},{10,14},{12... | collective-permute-start | bytes 86024 | tf_op jit(solution)/shard_map/ppermute | solution.py:393
  136.6 1.2 collective-permute-start.6
  138.5 1.1 collective-permute-done.6.refs_3_
  139.7 1.2 collective-permute-start.7
  140.9 2.5 %collective-permute-start.8 = (f32[1,8,896]{2,1,0:T(8,128)S(1)}, f32[1,8,896]{2,1,0:T(8,128)S(1)}, u32[]{:S(2)}, u32[]{:S(2)}) collective-permute-start(f32[1,8,896]{2,1,0:T(8,128)S(1)} %fold.4.refs_0_), channel_id=1, source_target_pairs={{0,16},{8,24},{16,0},{24,8},{1,17},{9,25},{17,1},{25,9},{2,18},{10... | collective-permute-start | bytes 86024 | tf_op jit(solution)/shard_map/ppermute | solution.py:393
  143.4 1.1 collective-permute-start.9
  144.6 1.4 copy.14
  146.3 3.5 %collective-permute-start.10 = (f32[1,8,768]{2,1,0:T(8,128)S(1)}, f32[1,8,768]{2,1,0:T(8,128)S(1)}, u32[]{:S(2)}, u32[]{:S(2)}) collective-permute-start(f32[1,8,768]{2,1,0:T(8,128)S(1)} %fold.5), channel_id=1, source_target_pairs={{0,1},{1,0},{2,3},{3,2},{4,5},{5,4},{6,7},{7,6},{8,9},{9,8},{10,11... | collective-permute-start | bytes 73736 | tf_op jit(solution)/shard_map/ppermute | solution.py:397
  149.8 1.3 pad_maximum_fusion
  (38 shorter events, 4.1 us)
Async XLA Ops:
  4.0 9.6 %copy-start.3 = (f32[768]{0:T(1024)S(1)}, f32[768]{0:T(1024)}, u32[]{:S(2)}) copy-start(f32[768]{0:T(1024)} %param.12) | copy-start | bytes 9220
  4.0 31.7 %copy-start.1 = (s32[2]{0:T(128)S(1)}, s32[2]{0:T(128)}, u32[]{:S(2)}) copy-start(s32[2]{0:T(128)} %counts_ref.11) | copy-start | bytes 28
  4.0 31.7 %all-to-all-start = ((bf16[32,2,16,768]{3,2,1,0:T(8,128)(2,1)}), bf16[32,2,16,768]{3,2,1,0:T(8,128)(2,1)S(1)}, u32[]{:S(2)}, u32[]{:S(2)}) async-start(bf16[32,2,16,768]{3,2,1,0:T(8,128)(2,1)} %bitcast.13.x_ref.refs_0_), calls=%async_computation | async-start | bytes 3145728 | tf_op jit(solution)/shard_map/all_to_all | solution.py:404
  48.3 5.7 %copy-start.5 = (bf16[192,768]{1,0:T(8,128)(2,1)S(1)}, bf16[192,768]{1,0:T(8,128)(2,1)}, u32[]{:S(2)}) copy-start(bf16[192,768]{1,0:T(8,128)(2,1)} %refs_7_.3) | copy-start | bytes 884740
  48.3 23.2 %all-to-all-start.1 = ((bf16[32,16,896]{2,1,0:T(8,128)(2,1)}), bf16[32,16,896]{2,1,0:T(8,128)(2,1)S(1)}, u32[]{:S(2)}, u32[]{:S(2)}) async-start(bf16[32,16,896]{2,1,0:T(8,128)(2,1)} %bitcast.20), calls=%async_computation.1 | async-start | bytes 1835008 | tf_op jit(solution)/shard_map/all_to_all | solution.py:404
  54.0 47.6 %collective-permute-start = (bf16[192,768]{1,0:T(8,128)(2,1)S(1)}, bf16[192,768]{1,0:T(8,128)(2,1)S(1)}, u32[]{:S(2)}, u32[]{:S(2)}) collective-permute-start(bf16[192,768]{1,0:T(8,128)(2,1)S(1)} %copy-done.5), channel_id=1, source_target_pairs={{0,32},{32,64},{64,96},{96,0},{1,33},{33,65},{65,97},{97,1},{2,34}... | collective-permute-start | bytes 884744 | tf_op jit(solution)/shard_map/ppermute | solution.py:432
  55.4 46.2 %collective-permute-start.1 = (bf16[192,768]{1,0:T(8,128)(2,1)S(1)}, bf16[192,768]{1,0:T(8,128)(2,1)S(1)}, u32[]{:S(2)}, u32[]{:S(2)}) collective-permute-start(bf16[192,768]{1,0:T(8,128)(2,1)S(1)} %copy-done.5), channel_id=1, source_target_pairs={{0,64},{32,96},{64,0},{96,32},{1,65},{33,97},{65,1},{97,33},{2,66}... | collective-permute-start | bytes 884744 | tf_op jit(solution)/shard_map/ppermute | solution.py:432
  58.0 43.6 %collective-permute-start.2 = (bf16[192,768]{1,0:T(8,128)(2,1)S(1)}, bf16[192,768]{1,0:T(8,128)(2,1)}, u32[]{:S(2)}, u32[]{:S(2)}) collective-permute-start(bf16[192,768]{1,0:T(8,128)(2,1)S(1)} %copy-done.5), channel_id=1, source_target_pairs={{0,96},{32,0},{64,32},{96,64},{1,97},{33,1},{65,33},{97,65},{2,98}... | collective-permute-start | bytes 884744 | tf_op jit(solution)/shard_map/ppermute | solution.py:432
  71.6 45.2 %all-to-all-start.2 = ((bf16[32,16,896]{2,1,0:T(8,128)(2,1)}), bf16[32,16,896]{2,1,0:T(8,128)(2,1)S(1)}, u32[]{:S(2)}, u32[]{:S(2)}) async-start(bf16[32,16,896]{2,1,0:T(8,128)(2,1)} %bitcast.19), calls=%async_computation.2 | async-start | bytes 1835008 | tf_op jit(solution)/shard_map/all_to_all | solution.py:404
  79.9 10.8 %copy-start.4 = (f32[768]{0:T(1024)S(1)}, f32[768]{0:T(1024)}, u32[]{:S(2)}) copy-start(f32[768]{0:T(1024)} %param.15) | copy-start | bytes 9220
  90.8 11.7 %copy-start = (f32[384,8]{0,1:T(8,128)S(1)}, f32[384,8]{0,1:T(8,128)}, u32[]{:S(2)}) copy-start(f32[384,8]{0,1:T(8,128)} %param.19) | copy-start | bytes 36868
  101.6 0.7 copy-start.6
  101.6 0.8 copy-start.7
  131.3 14.6 %copy-start.2 = (bf16[32,16,768]{2,1,0:T(8,128)(2,1)S(1)}, bf16[32,16,768]{2,1,0:T(8,128)(2,1)}, u32[]{:S(2)}) copy-start(bf16[32,16,768]{2,1,0:T(8,128)(2,1)} %get-tuple-element.6) | copy-start | bytes 2359300
  131.3 1.3 collective-permute-start.3
  132.8 5.0 %collective-permute-start.4 = (f32[1,8,896]{2,1,0:T(8,128)S(1)}, f32[1,8,896]{2,1,0:T(8,128)S(1)}, u32[]{:S(2)}, u32[]{:S(2)}) collective-permute-start(f32[1,8,896]{2,1,0:T(8,128)S(1)} %fold.3.refs_0_), channel_id=1, source_target_pairs={{0,2},{2,4},{4,6},{6,0},{1,3},{3,5},{5,7},{7,1},{8,10},{10,12},{12... | collective-permute-start | bytes 86024 | tf_op jit(solution)/shard_map/ppermute | solution.py:393
  134.2 4.3 %collective-permute-start.5 = (f32[1,8,896]{2,1,0:T(8,128)S(1)}, f32[1,8,896]{2,1,0:T(8,128)S(1)}, u32[]{:S(2)}, u32[]{:S(2)}) collective-permute-start(f32[1,8,896]{2,1,0:T(8,128)S(1)} %fold.3.refs_0_), channel_id=1, source_target_pairs={{0,4},{2,6},{4,0},{6,2},{1,5},{3,7},{5,1},{7,3},{8,12},{10,14},{12... | collective-permute-start | bytes 86024 | tf_op jit(solution)/shard_map/ppermute | solution.py:393
  136.6 3.0 %collective-permute-start.6 = (f32[1,8,896]{2,1,0:T(8,128)S(1)}, f32[1,8,896]{2,1,0:T(8,128)S(1)}, u32[]{:S(2)}, u32[]{:S(2)}) collective-permute-start(f32[1,8,896]{2,1,0:T(8,128)S(1)} %fold.3.refs_0_), channel_id=1, source_target_pairs={{0,6},{2,0},{4,2},{6,4},{1,7},{3,1},{5,3},{7,5},{8,14},{10,8},{12,... | collective-permute-start | bytes 86024 | tf_op jit(solution)/shard_map/ppermute | solution.py:393
  139.7 6.5 %collective-permute-start.7 = (f32[1,8,896]{2,1,0:T(8,128)S(1)}, f32[1,8,896]{2,1,0:T(8,128)S(1)}, u32[]{:S(2)}, u32[]{:S(2)}) collective-permute-start(f32[1,8,896]{2,1,0:T(8,128)S(1)} %fold.4.refs_0_), channel_id=1, source_target_pairs={{0,8},{8,16},{16,24},{24,0},{1,9},{9,17},{17,25},{25,1},{2,10},{10... | collective-permute-start | bytes 86024 | tf_op jit(solution)/shard_map/ppermute | solution.py:393
  140.9 5.2 %collective-permute-start.8 = (f32[1,8,896]{2,1,0:T(8,128)S(1)}, f32[1,8,896]{2,1,0:T(8,128)S(1)}, u32[]{:S(2)}, u32[]{:S(2)}) collective-permute-start(f32[1,8,896]{2,1,0:T(8,128)S(1)} %fold.4.refs_0_), channel_id=1, source_target_pairs={{0,16},{8,24},{16,0},{24,8},{1,17},{9,25},{17,1},{25,9},{2,18},{10... | collective-permute-start | bytes 86024 | tf_op jit(solution)/shard_map/ppermute | solution.py:393
  143.4 2.8 %collective-permute-start.9 = (f32[1,8,896]{2,1,0:T(8,128)S(1)}, f32[1,8,896]{2,1,0:T(8,128)S(1)}, u32[]{:S(2)}, u32[]{:S(2)}) collective-permute-start(f32[1,8,896]{2,1,0:T(8,128)S(1)} %fold.4.refs_0_), channel_id=1, source_target_pairs={{0,24},{8,0},{16,8},{24,16},{1,25},{9,1},{17,9},{25,17},{2,26},{10... | collective-permute-start | bytes 86024 | tf_op jit(solution)/shard_map/ppermute | solution.py:393
  146.3 4.8 %collective-permute-start.10 = (f32[1,8,768]{2,1,0:T(8,128)S(1)}, f32[1,8,768]{2,1,0:T(8,128)S(1)}, u32[]{:S(2)}, u32[]{:S(2)}) collective-permute-start(f32[1,8,768]{2,1,0:T(8,128)S(1)} %fold.5), channel_id=1, source_target_pairs={{0,1},{1,0},{2,3},{3,2},{4,5},{5,4},{6,7},{7,6},{8,9},{9,8},{10,11... | collective-permute-start | bytes 73736 | tf_op jit(solution)/shard_map/ppermute | solution.py:397
